TPU v7x, 32 devices: a whole 2x2x4 slice. The times are simulated.
32 devices in a mesh: cell: 8 (over y, x, core), gene: 4 (over z).
Axes of the slice: x: 2, y: 2, z: 4, core: 2. Of those that a mesh axis runs over, the one named last changes fastest.
Arguments:
- counts: int32 [2048, 2560], P('cell', 'gene'), may hold values from 1 to 8
- cell_factors: float32 [64, 2048], P(None, 'cell'), may hold values from -6 to 6
- loadings: float32 [64, 2560], P(None, 'gene'), may hold values from -3 to 3
- cell_momenta: float32 [64, 2048], P(None, 'cell'), may hold values from -6 to 6
- loading_momenta: float32 [64, 2560], P(None, 'gene'), may hold values from -6 to 6
- step: float32 [64], replicated, may hold values from 0.01 to 0.04
Outputs:
- new_factors: float32 [64, 2048], P(None, 'cell')
- new_loadings: float32 [64, 2560], P(None, 'gene')
- new_cell_momenta: float32 [64, 2048], P(None, 'cell')
- new_loading_momenta: float32 [64, 2560], P(None, 'gene')
- log_rate: bfloat16 [2048, 2560], P('cell', 'gene')
All inputs are finite; a program needn't handle non-finite values.
Results may differ from a plain program's by a relative error of at most 0.001.
Values sent between devices are 32-bit elements; how exact they have to be, the bound alone decides.
No kernel may reach another device: no remote copies, remote signals or barrier semaphores. Data moves between devices by JAX's collectives and lax.ppermute only.
A program may use at most 64 MiB of HBM per device.

v0:
```python
import functools

import jax
import jax.numpy as jnp
from jax import lax
from jax.experimental import pallas as pl
from jax.experimental.pallas import tpu as pltpu
from jax.sharding import PartitionSpec as P


PARAMS = pltpu.CompilerParams(vmem_limit_bytes=24 * 1024 * 1024)
PIECES = 4
FLOOR = 2.0**-100
VMEM = pl.BlockSpec(memory_space=pltpu.VMEM)
HBM = pl.BlockSpec(memory_space=pltpu.HBM)
SMEM = pl.BlockSpec(memory_space=pltpu.SMEM)
NT = (((1,), (1,)), ((), ()))
TN = (((0,), (0,)), ((), ()))
NN = (((1,), (0,)), ((), ()))


def dot(a, b, dims):
    return lax.dot_general(a, b, dims, preferred_element_type=jnp.float32)


def split(x):
    high = x.astype(jnp.bfloat16)
    return high, (x - high.astype(jnp.float32)).astype(jnp.bfloat16)


def weight_of(total):
    return jnp.clip(0.25 * total, FLOOR, 2.0**126)


def forward_math(scale, u, v, pack_ref, high_ref, low_ref):
    u_high, u_low = split(u * scale)
    v_high, v_low = split(v)
    linear = dot(
        jnp.concatenate([v_high, v_low, v_high, v_low], 0),
        jnp.concatenate([u_high, u_high, u_low, u_low], 0),
        TN,
    )
    expo = jnp.exp(linear)
    total = jnp.sum(expo, axis=0, keepdims=True)
    p_high, p_low = split(expo * (1.0 / weight_of(total)))
    high_ref[...] = p_high
    low_ref[...] = p_low
    ones = jnp.ones((16, v.shape[1]), jnp.bfloat16)
    s_high, s_low = split(v * v)
    squares = dot(ones, s_high, NT) + dot(ones, s_low, NT)
    pack_ref[...] = jnp.zeros(pack_ref.shape, jnp.float32)
    pack_ref[0:1, :] = total
    pack_ref[2:3, 0 : v.shape[0]] = squares[0:1]


def first_kernel(scale, counts_hbm, u_hbm, v_hbm, step_hbm, pack_ref, high_ref, low_ref, small_ref,
                 u_ref, v_ref, step_ref, counts_ref, sems):
    copies = [
        pltpu.make_async_copy(v_hbm, v_ref, sems.at[0]),
        pltpu.make_async_copy(u_hbm, u_ref, sems.at[1]),
    ]
    pieces = sems.shape[0] - 3
    rows = counts_ref.shape[0] // pieces
    for i in range(pieces):
        at = pl.ds(i * rows, rows)
        copies.append(
            pltpu.make_async_copy(counts_hbm.at[at, :], counts_ref.at[at, :], sems.at[2 + i])
        )
    copies.append(pltpu.make_async_copy(step_hbm, step_ref, sems.at[2 + pieces]))
    for copy in copies:
        copy.start()
    copies[0].wait()
    copies[1].wait()
    forward_math(scale, u_ref[...], v_ref[...], pack_ref, high_ref, low_ref)
    for copy in copies[2:]:
        copy.wait()
    small = counts_ref[...].astype(jnp.float32).astype(jnp.bfloat16)
    small_ref[...] = small
    ones = jnp.ones((16, small.shape[1]), jnp.bfloat16)
    pack_ref[1:2, :] = dot(ones, small, NT)[0:1]


def again_kernel(scale, u_ref, v_ref, *outs):
    forward_math(scale, u_ref[...], v_ref[...], *outs)


def forward_first(counts, u, v, step, scale):
    cells, genes = counts.shape
    shapes = [
        jax.ShapeDtypeStruct((8, cells), jnp.float32),
        jax.ShapeDtypeStruct((genes, cells), jnp.bfloat16),
        jax.ShapeDtypeStruct((genes, cells), jnp.bfloat16),
        jax.ShapeDtypeStruct((cells, genes), jnp.bfloat16),
        jax.ShapeDtypeStruct(u.shape, u.dtype),
        jax.ShapeDtypeStruct(v.shape, v.dtype),
        jax.ShapeDtypeStruct(step.shape, step.dtype),
    ]
    return pl.pallas_call(
        functools.partial(first_kernel, scale),
        out_shape=shapes,
        in_specs=[HBM] * 4,
        out_specs=[VMEM] * len(shapes),
        scratch_shapes=[
            pltpu.VMEM((cells, genes), counts.dtype),
            pltpu.SemaphoreType.DMA((3 + PIECES,)),
        ],
        name="forward_first",
        compiler_params=PARAMS,
    )(*(pltpu.with_memory_space_constraint(x, pltpu.HBM) for x in (counts, u, v, step)))


def forward_again(u, v, scale):
    cells, genes = u.shape[1], v.shape[1]
    shapes = [
        jax.ShapeDtypeStruct((8, cells), jnp.float32),
        jax.ShapeDtypeStruct((genes, cells), jnp.bfloat16),
        jax.ShapeDtypeStruct((genes, cells), jnp.bfloat16),
    ]
    return pl.pallas_call(
        functools.partial(again_kernel, scale),
        out_shape=shapes,
        in_specs=[VMEM] * 2,
        out_specs=[VMEM] * len(shapes),
        name="forward_again",
        compiler_params=PARAMS,
    )(u, v)


def products_kernel(scale, counts_ref, v_ref, high_ref, low_ref, out_ref):
    k = v_ref.shape[0]
    w_high, w_low = split(v_ref[...] * scale)
    both = jnp.concatenate([w_high, w_low], 0)
    data = dot(both, counts_ref[...], NT)
    mean = dot(both, high_ref[...], NN)
    out_ref[0:k, :] = data[:k] + data[k:]
    out_ref[k:, :] = mean[:k] + mean[k:] + dot(w_high, low_ref[...], NN)


def products(counts, v, high, low, scale):
    return pl.pallas_call(
        functools.partial(products_kernel, scale),
        out_shape=jax.ShapeDtypeStruct((2 * v.shape[0], counts.shape[0]), jnp.float32),
        in_specs=[VMEM] * 4,
        out_specs=VMEM,
        name="products",
        compiler_params=PARAMS,
    )(counts, v, high, low)


def rates_kernel(scale, u_ref, v_ref, size_ref, out_ref):
    u_high, u_low = split(u_ref[...] * scale)
    v_high, v_low = split(v_ref[...])
    linear = dot(
        jnp.concatenate([u_high, u_high, u_low, u_low], 0),
        jnp.concatenate([v_high, v_low, v_high, v_low], 0),
        TN,
    )
    log = jnp.log(size_ref[...])
    log_high, log_low = split(log)
    log_least = (log - log_high.astype(jnp.float32) - log_low.astype(jnp.float32)).astype(
        jnp.bfloat16
    )
    row = lax.broadcasted_iota(jnp.int32, (16, log.shape[1]), 0)
    terms = jnp.zeros((16, log.shape[1]), jnp.float32)
    for i, term in enumerate((log_high, log_low, log_least)):
        terms = jnp.where(row == i, term.astype(jnp.float32), terms)
    ones = jnp.ones((16, v_ref.shape[1]), jnp.bfloat16)
    shift = dot(terms.astype(jnp.bfloat16), ones, TN)
    out_ref[...] = (linear + shift).astype(jnp.bfloat16)


def rates_of(u, v, size, scale):
    return pl.pallas_call(
        functools.partial(rates_kernel, scale),
        out_shape=jax.ShapeDtypeStruct((u.shape[1], v.shape[1]), jnp.bfloat16),
        in_specs=[VMEM] * 3,
        out_specs=VMEM,
        name="rates",
        compiler_params=PARAMS,
    )(u, v, size)


def data_kernel(scale, counts_ref, u_ref, out_ref):
    k = u_ref.shape[0]
    u_high, u_low = split(u_ref[...] * scale)
    both = dot(jnp.concatenate([u_high, u_low], 0), counts_ref[...], NN)
    out_ref[...] = both[:k] + both[k:]


def data_part(counts, u, scale):
    return pl.pallas_call(
        functools.partial(data_kernel, scale),
        out_shape=jax.ShapeDtypeStruct((u.shape[0], counts.shape[1]), jnp.float32),
        in_specs=[VMEM] * 2,
        out_specs=VMEM,
        name="data_part",
        compiler_params=PARAMS,
    )(counts, u)


def part_kernel(scale, at_ref, u_ref, size_ref, data_ref, high_ref, low_ref, out_ref):
    hk = out_ref.shape[0]
    rows = pl.ds(pl.multiple_of(at_ref[0], hk), hk)
    u_high, u_low = split(u_ref[rows, :] * size_ref[...] * scale)
    both = dot(jnp.concatenate([u_high, u_low], 0), high_ref[...], NT)
    rest = dot(u_high, low_ref[...], NT)
    out_ref[...] = data_ref[rows, :] - (both[:hk] + both[hk:] + rest)


def part(at, u, size, data, high, low, scale):
    return pl.pallas_call(
        functools.partial(part_kernel, scale),
        out_shape=jax.ShapeDtypeStruct((u.shape[0] // 2, high.shape[0]), jnp.float32),
        in_specs=[SMEM] + [VMEM] * 5,
        out_specs=VMEM,
        compiler_params=PARAMS,
    )(at, u, size, data, high, low)


def finish_kernel(at_ref, own_ref, other_ref, u_ref, u_hbm, v_hbm, sems):
    hk = own_ref.shape[0]
    first = pl.multiple_of(at_ref[0], hk)
    copies = (
        pltpu.make_async_copy(u_ref, u_hbm, sems.at[0]),
        pltpu.make_async_copy(own_ref, v_hbm.at[pl.ds(first, hk), :], sems.at[1]),
        pltpu.make_async_copy(other_ref, v_hbm.at[pl.ds(hk - first, hk), :], sems.at[2]),
    )
    for copy in copies:
        copy.start()
    for copy in copies:
        copy.wait()


def finish(at, own, other, u):
    hk, genes = own.shape
    return pl.pallas_call(
        finish_kernel,
        out_shape=(
            jax.ShapeDtypeStruct(u.shape, u.dtype),
            jax.ShapeDtypeStruct((2 * hk, genes), own.dtype),
        ),
        in_specs=[SMEM] + [VMEM] * 3,
        out_specs=(HBM, HBM),
        scratch_shapes=[pltpu.SemaphoreType.DMA((3,))],
        name="finish",
        compiler_params=PARAMS,
    )(at, own, other, u)


def swap(x, axis, bits):
    n = lax.axis_size(axis)
    return lax.ppermute(x, axis, [(j, j ^ bits) for j in range(n)])


def stages(lo, n):
    out = []
    bit = lo
    while bit < n:
        out.append([bit, 2 * bit, 3 * bit] if 4 * bit <= n else [bit])
        bit *= 4
    return out


def exchange_sum(x, axis, lo):
    for group in stages(lo, lax.axis_size(axis)):
        parts = [swap(x, axis, bits) for bits in group]
        for got in parts:
            x = x + got
    return x


def local(counts, cell_factors, loadings, cell_momenta, loading_momenta, step):
    k, _ = cell_factors.shape
    scale = 1.0 / k**0.5
    n_gene = lax.axis_size("gene")
    genes_total = jnp.float32(loadings.shape[1] * n_gene)
    hk = k // 2
    side = lax.axis_index("cell") % 2
    at_own = jnp.reshape(side * hk, (1,)).astype(jnp.int32)
    at_send = hk - at_own

    def mine(x):
        return lax.dynamic_slice_in_dim(x, side * hk, hk, 0)

    def join(x):
        y = swap(x, "cell", 1)
        first = side == 0
        return jnp.concatenate([jnp.where(first, x, y), jnp.where(first, y, x)], 0)

    def gather(wide, pack):
        got = swap(wide, "gene", 1)
        parts = [swap(pack, "gene", bits) for bits in stages(1, n_gene)[0]]
        near = parts[0]
        whole = pack
        for more in parts:
            whole = whole + more
        if n_gene > 4:
            whole = exchange_sum(whole, "gene", 4)
        return got, near, whole

    def cross_of(wide, got, pack, near, size):
        own_size = size * weight_of(pack[0:1])
        near_size = size * weight_of(near[0:1])
        cross = (wide[:k] + got[:k]) - own_size * wide[k : 2 * k] - near_size * got[k : 2 * k]
        bit = 2
        while bit < n_gene:
            cross = cross + swap(cross, "gene", bit)
            bit *= 2
        return cross, own_size

    def gradient(counts_in, factors, loads, own, library):
        first = library is None
        pace = None
        if first:
            pack, high, low, counts_in, factors, loads, pace = forward_first(
                counts_in, factors, loads, step[None], scale
            )
        else:
            pack, high, low = forward_again(factors, loads, scale)
        wide = products(counts_in, loads, high, low, scale)
        got, near, whole = gather(wide, pack)
        data = data_part(counts_in, factors, scale)
        library = whole[1:2] if first else library
        size = library / whole[0:1]
        cross, own_size = cross_of(wide, got, pack, near, size)
        send = part(at_send, factors, own_size, data, high, low, scale)
        back = swap(send, "cell", 1)
        kept = part(at_own, factors, own_size, data, high, low, scale)
        total = exchange_sum(back + kept, "cell", 2)
        ard = (genes_total + 2.0) / (whole[2, :k] + 2.0)
        own = mine(loads) if first else own
        grad_v = total - mine(ard[:, None]) * own
        return cross - factors, grad_v, library, size, counts_in, factors, own, pace

    mom_v = mine(loading_momenta)
    grad_u, grad_v, library, size, counts_small, factors, own, pace = gradient(
        counts, cell_factors, loadings, None, None
    )
    full = jnp.reshape(pace, (k, 1))
    full_own = mine(full)
    half, half_own = 0.5 * full, 0.5 * full_own
    mom_u = cell_momenta + half * grad_u
    mom_v = mom_v + half_own * grad_v
    factors = factors + full * mom_u
    own = own + full_own * mom_v
    loads = join(own)
    grad_u, grad_v, library, size, *_ = gradient(
        counts_small, factors, loads, own, library
    )
    rates = rates_of(factors, loads, size, scale)
    mom_u = mom_u + half * grad_u
    own_mom = mom_v + half_own * grad_v
    mom_u, mom_v = finish(at_own, own_mom, swap(own_mom, "cell", 1), mom_u)
    return (factors, loads, mom_u, mom_v, rates)


def solution(mesh):
    placed = (
        P("cell", "gene"),
        P(None, "cell"),
        P(None, "gene"),
        P(None, "cell"),
        P(None, "gene"),
        P(),
    )
    return jax.shard_map(
        local,
        mesh=mesh,
        in_specs=placed,
        out_specs=(
            P(None, "cell"),
            P(None, "gene"),
            P(None, "cell"),
            P(None, "gene"),
            P("cell", "gene"),
        ),
        check_vma=False,
    )
```

profile of v0, /device:TPU:0, one launch (start us, length us, event | category | flops | bytes accessed | tf_op | source)
XLA Modules:
  0.0 42.7 jit_solution(16781906648772853592)
XLA Ops:
  0.6 1.7 %forward_first.1 = (f32[8,256]{1,0:T(8,128)S(1)}, bf16[640,256]{1,0:T(8,128)(2,1)S(1)}, bf16[640,256]{1,0:T(8,128)(2,1)S(1)}, bf16[256,640]{1,0:T(8,128)(2,1)S(1...) custom-call(s32[256,640]{1,0:T(8,128)} %counts_hbm.1, f32[64,256]{1,0:T(8,128)} %u_hbm.1, ...), custom_call_target="tpu_custom_call" | custom-call | tf_op jit(solution)/shard_map/forward_first/pallas_call | solution.py:98
  2.4 5.1 %collective-permute-start.3 = (f32[8,256]{1,0:T(8,128)S(1)}, f32[8,256]{1,0:T(8,128)S(1)}, u32[]{:S(2)}, u32[]{:S(2)}) collective-permute-start(f32[8,256]{1,0:T(8,128)S(1)} %get-tuple-element.23), channel_id=1, source_target_pairs={{0,3},{1,2},{2,1},{3,0},{4,7},{5,6},{6,5},{7,4},{8,11},{9,10},{10,... | collective-permute-start | bytes 24584 | tf_op jit(solution)/shard_map/ppermute | solution.py:252
  7.5 0.0 collective-permute-start.2
  7.5 0.6 %collective-permute-start.1 = (f32[8,256]{1,0:T(8,128)S(1)}, f32[8,256]{1,0:T(8,128)S(1)}, u32[]{:S(2)}, u32[]{:S(2)}) collective-permute-start(f32[8,256]{1,0:T(8,128)S(1)} %get-tuple-element.23), channel_id=1, source_target_pairs={{0,1},{1,0},{2,3},{3,2},{4,5},{5,4},{6,7},{7,6},{8,9},{9,8},{10,11... | collective-permute-start | bytes 24584 | tf_op jit(solution)/shard_map/ppermute | solution.py:252
  8.2 0.3 products.2
  8.5 1.4 %collective-permute-start = (f32[128,256]{1,0:T(8,128)S(1)}, f32[128,256]{1,0:T(8,128)S(1)}, u32[]{:S(2)}, u32[]{:S(2)}) collective-permute-start(f32[128,256]{1,0:T(8,128)S(1)} %products.2), channel_id=1, source_target_pairs={{0,1},{1,0},{2,3},{3,2},{4,5},{5,4},{6,7},{7,6},{8,9},{9,8},{10,11... | collective-permute-start | bytes 393224 | tf_op jit(solution)/shard_map/ppermute | solution.py:252
  10.0 0.1 broadcast_multiply_fusion
  10.0 0.2 data_part.2.data_ref
  10.3 0.0 collective-permute-done.3
  10.3 1.8 %collective-permute-done.2 = f32[8,256]{1,0:T(8,128)S(1)} collective-permute-done((f32[8,256]{1,0:T(8,128)S(1)}, f32[8,256]{1,0:T(8,128)S(1)}, u32[]{:S(2)}, u32[]{:S(2)}) %collective-permute-start.2) | collective-permute-done | bytes 8224 | tf_op jit(solution)/shard_map/ppermute | solution.py:252
  12.1 0.0 collective-permute-done.1
  12.1 0.3 shard_map.101
  12.4 0.1 collective-permute-start.5
  12.5 0.3 shard_map.102
  12.8 0.1 fusion.9
  12.9 0.9 %collective-permute-done.5 = f32[32,640]{1,0:T(8,128)S(1)} collective-permute-done((f32[32,640]{1,0:T(8,128)S(1)}, f32[32,640]{1,0:T(8,128)S(1)}, u32[]{:S(2)}, u32[]{:S(2)}) %collective-permute-start.5) | collective-permute-done | bytes 81952 | tf_op jit(solution)/shard_map/ppermute | solution.py:252
  13.8 2.5 %collective-permute-start.8 = (f32[32,640]{1,0:T(8,128)S(1)}, f32[32,640]{1,0:T(8,128)S(1)}, u32[]{:S(2)}, u32[]{:S(2)}) collective-permute-start(f32[32,640]{1,0:T(8,128)S(1)} %add.100), channel_id=1, source_target_pairs={{0,24},{4,28},{8,16},{12,20},{16,8},{20,12},{24,0},{28,4},{1,25},{... | collective-permute-start | bytes 245768 | tf_op jit(solution)/shard_map/ppermute | solution.py:252
  16.3 0.5 %collective-permute-start.7 = (f32[32,640]{1,0:T(8,128)S(1)}, f32[32,640]{1,0:T(8,128)S(1)}, u32[]{:S(2)}, u32[]{:S(2)}) collective-permute-start(f32[32,640]{1,0:T(8,128)S(1)} %add.100), channel_id=1, source_target_pairs={{0,16},{4,20},{8,24},{12,28},{16,0},{20,4},{24,8},{28,12},{1,17},{... | collective-permute-start | bytes 245768 | tf_op jit(solution)/shard_map/ppermute | solution.py:252
  16.8 0.5 %collective-permute-start.6 = (f32[32,640]{1,0:T(8,128)S(1)}, f32[32,640]{1,0:T(8,128)S(1)}, u32[]{:S(2)}, u32[]{:S(2)}) collective-permute-start(f32[32,640]{1,0:T(8,128)S(1)} %add.100), channel_id=1, source_target_pairs={{0,8},{4,12},{8,0},{12,4},{16,24},{20,28},{24,16},{28,20},{1,9},{5... | collective-permute-start | bytes 245768 | tf_op jit(solution)/shard_map/ppermute | solution.py:252
  17.3 0.0 collective-permute-done
  17.4 2.1 %collective-permute-start.4 = (f32[64,256]{1,0:T(8,128)S(1)}, f32[64,256]{1,0:T(8,128)S(1)}, u32[]{:S(2)}, u32[]{:S(2)}) collective-permute-start(f32[64,256]{1,0:T(8,128)S(1)} %fusion.2), channel_id=1, source_target_pairs={{0,2},{1,3},{2,0},{3,1},{4,6},{5,7},{6,4},{7,5},{8,10},{9,11},{10,... | collective-permute-start | bytes 196616 | tf_op jit(solution)/shard_map/ppermute | solution.py:252
  19.5 0.0 collective-permute-done.8
  19.5 1.5 %collective-permute-done.7 = f32[32,640]{1,0:T(8,128)S(1)} collective-permute-done((f32[32,640]{1,0:T(8,128)S(1)}, f32[32,640]{1,0:T(8,128)S(1)}, u32[]{:S(2)}, u32[]{:S(2)}) %collective-permute-start.7) | collective-permute-done | bytes 81952 | tf_op jit(solution)/shard_map/ppermute | solution.py:252
  21.0 0.2 collective-permute-done.6
  21.3 0.0 copy-done.3
  21.3 0.1 multiply_add_fusion.1
  21.4 0.1 collective-permute-start.9
  21.4 1.2 %collective-permute-done.4 = f32[64,256]{1,0:T(8,128)S(1)} collective-permute-done((f32[64,256]{1,0:T(8,128)S(1)}, f32[64,256]{1,0:T(8,128)S(1)}, u32[]{:S(2)}, u32[]{:S(2)}) %collective-permute-start.4) | collective-permute-done | bytes 65568 | tf_op jit(solution)/shard_map/ppermute | solution.py:252
  22.6 0.0 copy-done.2
  22.6 0.1 multiply_add_fusion.4.u_ref
  22.7 0.0 copy-start
  22.7 0.0 collective-permute-done.9
  22.8 0.0 copy-start.1
  22.8 0.5 %forward_again.1 = (f32[8,256]{1,0:T(8,128)S(1)}, bf16[640,256]{1,0:T(8,128)(2,1)S(1)}, bf16[640,256]{1,0:T(8,128)(2,1)S(1)}) custom-call(f32[64,256]{1,0:T(8,128)S(1)} %multiply_add_fusion.4.u_ref, f32[64,640]{1,0:T(8,128)S(1)} %pad_maximum_fusion.v_ref), custom_call_target="tpu_custom_call" | custom-call | tf_op jit(solution)/shard_map/forward_again/pallas_call | solution.py:119
  23.3 2.1 %collective-permute-start.12 = (f32[8,256]{1,0:T(8,128)S(1)}, f32[8,256]{1,0:T(8,128)S(1)}, u32[]{:S(2)}, u32[]{:S(2)}) collective-permute-start(f32[8,256]{1,0:T(8,128)S(1)} %get-tuple-element.24), channel_id=1, source_target_pairs={{0,3},{1,2},{2,1},{3,0},{4,7},{5,6},{6,5},{7,4},{8,11},{9,10},{10,... | collective-permute-start | bytes 24584 | tf_op jit(solution)/shard_map/ppermute | solution.py:252
  25.4 0.1 collective-permute-start.11
  25.5 2.2 %collective-permute-start.10 = (f32[8,256]{1,0:T(8,128)S(1)}, f32[8,256]{1,0:T(8,128)S(1)}, u32[]{:S(2)}, u32[]{:S(2)}) collective-permute-start(f32[8,256]{1,0:T(8,128)S(1)} %get-tuple-element.24), channel_id=1, source_target_pairs={{0,1},{1,0},{2,3},{3,2},{4,5},{5,4},{6,7},{7,6},{8,9},{9,8},{10,11... | collective-permute-start | bytes 24584 | tf_op jit(solution)/shard_map/ppermute | solution.py:252
  27.8 0.2 data_part.3.data_ref
  28.0 0.3 products.3
  28.3 0.1 collective-permute-start.18
  28.4 0.5 %collective-permute-done.12 = f32[8,256]{1,0:T(8,128)S(1)} collective-permute-done((f32[8,256]{1,0:T(8,128)S(1)}, f32[8,256]{1,0:T(8,128)S(1)}, u32[]{:S(2)}, u32[]{:S(2)}) %collective-permute-start.12) | collective-permute-done | bytes 8224 | tf_op jit(solution)/shard_map/ppermute | solution.py:252
  28.9 1.1 %collective-permute-done.11 = f32[8,256]{1,0:T(8,128)S(1)} collective-permute-done((f32[8,256]{1,0:T(8,128)S(1)}, f32[8,256]{1,0:T(8,128)S(1)}, u32[]{:S(2)}, u32[]{:S(2)}) %collective-permute-start.11) | collective-permute-done | bytes 8224 | tf_op jit(solution)/shard_map/ppermute | solution.py:252
  30.0 0.0 collective-permute-done.10
  30.0 0.3 shard_map.103
  30.3 0.3 shard_map.104
  30.6 0.0 copy-done.1
  30.6 1.1 %rates.1 = bf16[256,640]{1,0:T(8,128)(2,1)} custom-call(f32[64,256]{1,0:T(8,128)S(1)} %multiply_add_fusion.4.u_ref, f32[64,640]{1,0:T(8,128)S(1)} %pad_maximum_fusion.v_ref, f32[1,256]{1,0:T(1,128)S(1)} %get-tuple-element.30.size_ref), custom_call_target="tpu_custom_call" | custom-call | tf_op jit(solution)/shard_map/rates/pallas_call | solution.py:173
  31.7 0.0 collective-permute-start.13
  31.8 0.1 fusion.10
  31.8 1.2 %collective-permute-done.13 = f32[32,640]{1,0:T(8,128)S(1)} collective-permute-done((f32[32,640]{1,0:T(8,128)S(1)}, f32[32,640]{1,0:T(8,128)S(1)}, u32[]{:S(2)}, u32[]{:S(2)}) %collective-permute-start.13) | collective-permute-done | bytes 81952 | tf_op jit(solution)/shard_map/ppermute | solution.py:252
  33.0 2.6 %collective-permute-start.16 = (f32[32,640]{1,0:T(8,128)S(1)}, f32[32,640]{1,0:T(8,128)S(1)}, u32[]{:S(2)}, u32[]{:S(2)}) collective-permute-start(f32[32,640]{1,0:T(8,128)S(1)} %add.110), channel_id=1, source_target_pairs={{0,24},{4,28},{8,16},{12,20},{16,8},{20,12},{24,0},{28,4},{1,25},{... | collective-permute-start | bytes 245768 | tf_op jit(solution)/shard_map/ppermute | solution.py:252
  35.6 0.4 collective-permute-start.15
  36.1 0.5 %collective-permute-start.14 = (f32[32,640]{1,0:T(8,128)S(1)}, f32[32,640]{1,0:T(8,128)S(1)}, u32[]{:S(2)}, u32[]{:S(2)}) collective-permute-start(f32[32,640]{1,0:T(8,128)S(1)} %add.110), channel_id=1, source_target_pairs={{0,8},{4,12},{8,0},{12,4},{16,24},{20,28},{24,16},{28,20},{1,9},{5... | collective-permute-start | bytes 245768 | tf_op jit(solution)/shard_map/ppermute | solution.py:252
  36.6 0.0 collective-permute-done.18
  36.6 2.2 %collective-permute-start.19 = (f32[64,256]{1,0:T(8,128)S(1)}, f32[64,256]{1,0:T(8,128)S(1)}, u32[]{:S(2)}, u32[]{:S(2)}) collective-permute-start(f32[64,256]{1,0:T(8,128)S(1)} %fusion), channel_id=1, source_target_pairs={{0,2},{1,3},{2,0},{3,1},{4,6},{5,7},{6,4},{7,5},{8,10},{9,11},{10,... | collective-permute-start | bytes 196616 | tf_op jit(solution)/shard_map/ppermute | solution.py:252
  38.8 0.0 collective-permute-done.16
  38.8 1.5 %collective-permute-done.15 = f32[32,640]{1,0:T(8,128)S(1)} collective-permute-done((f32[32,640]{1,0:T(8,128)S(1)}, f32[32,640]{1,0:T(8,128)S(1)}, u32[]{:S(2)}, u32[]{:S(2)}) %collective-permute-start.15) | collective-permute-done | bytes 81952 | tf_op jit(solution)/shard_map/ppermute | solution.py:252
  40.3 0.2 collective-permute-done.14
  40.5 0.1 multiply_add_fusion.own_ref
  40.6 0.1 collective-permute-start.17
  40.7 1.2 %collective-permute-done.19 = f32[64,256]{1,0:T(8,128)S(1)} collective-permute-done((f32[64,256]{1,0:T(8,128)S(1)}, f32[64,256]{1,0:T(8,128)S(1)}, u32[]{:S(2)}, u32[]{:S(2)}) %collective-permute-start.19) | collective-permute-done | bytes 65568 | tf_op jit(solution)/shard_map/ppermute | solution.py:252
  41.9 0.1 multiply_add_fusion.3.u_ref
  42.0 0.0 collective-permute-done.17.other_ref
  42.0 0.7 %finish.1 = (f32[64,256]{1,0:T(8,128)}, f32[64,640]{1,0:T(8,128)}) custom-call(s32[1]{0:T(128)} %bitcast.5.at_ref, f32[32,640]{1,0:T(8,128)S(1)} %multiply_add_fusion.own_ref, f32[32,640]{1,0:T(8,128)S(1)} %collective-permute-done.17.other_ref, f32[64,256]{1,0:T(8,128)S(1)} %multiply_add_fusion.3.u_ref), custom_call_target="tpu_custom_call" | custom-call | tf_op jit(solution)/shard_map/finish/pallas_call | solution.py:236
  (18 shorter events, 0.2 us)
Async XLA Ops:
  2.4 7.9 %collective-permute-start.3 = (f32[8,256]{1,0:T(8,128)S(1)}, f32[8,256]{1,0:T(8,128)S(1)}, u32[]{:S(2)}, u32[]{:S(2)}) collective-permute-start(f32[8,256]{1,0:T(8,128)S(1)} %get-tuple-element.23), channel_id=1, source_target_pairs={{0,3},{1,2},{2,1},{3,0},{4,7},{5,6},{6,5},{7,4},{8,11},{9,10},{10,... | collective-permute-start | bytes 24584 | tf_op jit(solution)/shard_map/ppermute | solution.py:252
  7.5 4.6 %collective-permute-start.2 = (f32[8,256]{1,0:T(8,128)S(1)}, f32[8,256]{1,0:T(8,128)S(1)}, u32[]{:S(2)}, u32[]{:S(2)}) collective-permute-start(f32[8,256]{1,0:T(8,128)S(1)} %get-tuple-element.23), channel_id=1, source_target_pairs={{0,2},{1,3},{2,0},{3,1},{4,6},{5,7},{6,4},{7,5},{8,10},{9,11},{10,... | collective-permute-start | bytes 24584 | tf_op jit(solution)/shard_map/ppermute | solution.py:252
  7.5 4.6 %collective-permute-start.1 = (f32[8,256]{1,0:T(8,128)S(1)}, f32[8,256]{1,0:T(8,128)S(1)}, u32[]{:S(2)}, u32[]{:S(2)}) collective-permute-start(f32[8,256]{1,0:T(8,128)S(1)} %get-tuple-element.23), channel_id=1, source_target_pairs={{0,1},{1,0},{2,3},{3,2},{4,5},{5,4},{6,7},{7,6},{8,9},{9,8},{10,11... | collective-permute-start | bytes 24584 | tf_op jit(solution)/shard_map/ppermute | solution.py:252
  8.5 8.8 %collective-permute-start = (f32[128,256]{1,0:T(8,128)S(1)}, f32[128,256]{1,0:T(8,128)S(1)}, u32[]{:S(2)}, u32[]{:S(2)}) collective-permute-start(f32[128,256]{1,0:T(8,128)S(1)} %products.2), channel_id=1, source_target_pairs={{0,1},{1,0},{2,3},{3,2},{4,5},{5,4},{6,7},{7,6},{8,9},{9,8},{10,11... | collective-permute-start | bytes 393224 | tf_op jit(solution)/shard_map/ppermute | solution.py:252
  12.4 1.4 %collective-permute-start.5 = (f32[32,640]{1,0:T(8,128)S(1)}, f32[32,640]{1,0:T(8,128)S(1)}, u32[]{:S(2)}, u32[]{:S(2)}) collective-permute-start(f32[32,640]{1,0:T(8,128)S(1)} %shard_map.101), channel_id=1, source_target_pairs={{0,4},{4,0},{8,12},{12,8},{16,20},{20,16},{24,28},{28,24},{1,5},{5... | collective-permute-start | bytes 245768 | tf_op jit(solution)/shard_map/ppermute | solution.py:252
  13.8 5.7 %collective-permute-start.8 = (f32[32,640]{1,0:T(8,128)S(1)}, f32[32,640]{1,0:T(8,128)S(1)}, u32[]{:S(2)}, u32[]{:S(2)}) collective-permute-start(f32[32,640]{1,0:T(8,128)S(1)} %add.100), channel_id=1, source_target_pairs={{0,24},{4,28},{8,16},{12,20},{16,8},{20,12},{24,0},{28,4},{1,25},{... | collective-permute-start | bytes 245768 | tf_op jit(solution)/shard_map/ppermute | solution.py:252
  16.3 4.7 %collective-permute-start.7 = (f32[32,640]{1,0:T(8,128)S(1)}, f32[32,640]{1,0:T(8,128)S(1)}, u32[]{:S(2)}, u32[]{:S(2)}) collective-permute-start(f32[32,640]{1,0:T(8,128)S(1)} %add.100), channel_id=1, source_target_pairs={{0,16},{4,20},{8,24},{12,28},{16,0},{20,4},{24,8},{28,12},{1,17},{... | collective-permute-start | bytes 245768 | tf_op jit(solution)/shard_map/ppermute | solution.py:252
  16.8 4.4 %collective-permute-start.6 = (f32[32,640]{1,0:T(8,128)S(1)}, f32[32,640]{1,0:T(8,128)S(1)}, u32[]{:S(2)}, u32[]{:S(2)}) collective-permute-start(f32[32,640]{1,0:T(8,128)S(1)} %add.100), channel_id=1, source_target_pairs={{0,8},{4,12},{8,0},{12,4},{16,24},{20,28},{24,16},{28,20},{1,9},{5... | collective-permute-start | bytes 245768 | tf_op jit(solution)/shard_map/ppermute | solution.py:252
  17.3 3.9 %copy-start.3 = (f32[64,640]{1,0:T(8,128)S(1)}, f32[64,640]{1,0:T(8,128)}, u32[]{:S(2)}) copy-start(f32[64,640]{1,0:T(8,128)} %param.10) | copy-start | bytes 491524
  17.4 5.2 %collective-permute-start.4 = (f32[64,256]{1,0:T(8,128)S(1)}, f32[64,256]{1,0:T(8,128)S(1)}, u32[]{:S(2)}, u32[]{:S(2)}) collective-permute-start(f32[64,256]{1,0:T(8,128)S(1)} %fusion.2), channel_id=1, source_target_pairs={{0,2},{1,3},{2,0},{3,1},{4,6},{5,7},{6,4},{7,5},{8,10},{9,11},{10,... | collective-permute-start | bytes 196616 | tf_op jit(solution)/shard_map/ppermute | solution.py:252
  21.3 1.3 %copy-start.2 = (f32[64,256]{1,0:T(8,128)S(1)}, f32[64,256]{1,0:T(8,128)}, u32[]{:S(2)}) copy-start(f32[64,256]{1,0:T(8,128)} %param.9) | copy-start | bytes 196612
  21.4 1.4 %collective-permute-start.9 = (f32[32,640]{1,0:T(8,128)S(1)}, f32[32,640]{1,0:T(8,128)S(1)}, u32[]{:S(2)}, u32[]{:S(2)}) collective-permute-start(f32[32,640]{1,0:T(8,128)S(1)} %get-tuple-element.31), channel_id=1, source_target_pairs={{0,4},{4,0},{8,12},{12,8},{16,20},{20,16},{24,28},{28,24},{1,5},{5... | collective-permute-start | bytes 245768 | tf_op jit(solution)/shard_map/ppermute | solution.py:252
  22.7 19.2 %copy-start = (f32[64,256]{1,0:T(8,128)}, f32[64,256]{1,0:T(8,128)S(1)}, u32[]{:S(2)}) copy-start(f32[64,256]{1,0:T(8,128)S(1)} %multiply_add_fusion.4.u_ref) | copy-start | bytes 196612
  22.8 7.9 %copy-start.1 = (f32[64,640]{1,0:T(8,128)}, f32[64,640]{1,0:T(8,128)S(1)}, u32[]{:S(2)}) copy-start(f32[64,640]{1,0:T(8,128)S(1)} %pad_maximum_fusion.v_ref) | copy-start | bytes 491524
  23.3 5.6 %collective-permute-start.12 = (f32[8,256]{1,0:T(8,128)S(1)}, f32[8,256]{1,0:T(8,128)S(1)}, u32[]{:S(2)}, u32[]{:S(2)}) collective-permute-start(f32[8,256]{1,0:T(8,128)S(1)} %get-tuple-element.24), channel_id=1, source_target_pairs={{0,3},{1,2},{2,1},{3,0},{4,7},{5,6},{6,5},{7,4},{8,11},{9,10},{10,... | collective-permute-start | bytes 24584 | tf_op jit(solution)/shard_map/ppermute | solution.py:252
  25.4 4.6 %collective-permute-start.11 = (f32[8,256]{1,0:T(8,128)S(1)}, f32[8,256]{1,0:T(8,128)S(1)}, u32[]{:S(2)}, u32[]{:S(2)}) collective-permute-start(f32[8,256]{1,0:T(8,128)S(1)} %get-tuple-element.24), channel_id=1, source_target_pairs={{0,2},{1,3},{2,0},{3,1},{4,6},{5,7},{6,4},{7,5},{8,10},{9,11},{10,... | collective-permute-start | bytes 24584 | tf_op jit(solution)/shard_map/ppermute | solution.py:252
  25.5 4.4 %collective-permute-start.10 = (f32[8,256]{1,0:T(8,128)S(1)}, f32[8,256]{1,0:T(8,128)S(1)}, u32[]{:S(2)}, u32[]{:S(2)}) collective-permute-start(f32[8,256]{1,0:T(8,128)S(1)} %get-tuple-element.24), channel_id=1, source_target_pairs={{0,1},{1,0},{2,3},{3,2},{4,5},{5,4},{6,7},{7,6},{8,9},{9,8},{10,11... | collective-permute-start | bytes 24584 | tf_op jit(solution)/shard_map/ppermute | solution.py:252
  28.3 8.3 %collective-permute-start.18 = (f32[128,256]{1,0:T(8,128)S(1)}, f32[128,256]{1,0:T(8,128)S(1)}, u32[]{:S(2)}, u32[]{:S(2)}) collective-permute-start(f32[128,256]{1,0:T(8,128)S(1)} %products.3), channel_id=1, source_target_pairs={{0,1},{1,0},{2,3},{3,2},{4,5},{5,4},{6,7},{7,6},{8,9},{9,8},{10,11... | collective-permute-start | bytes 393224 | tf_op jit(solution)/shard_map/ppermute | solution.py:252
  31.7 1.3 %collective-permute-start.13 = (f32[32,640]{1,0:T(8,128)S(1)}, f32[32,640]{1,0:T(8,128)S(1)}, u32[]{:S(2)}, u32[]{:S(2)}) collective-permute-start(f32[32,640]{1,0:T(8,128)S(1)} %shard_map.103), channel_id=1, source_target_pairs={{0,4},{4,0},{8,12},{12,8},{16,20},{20,16},{24,28},{28,24},{1,5},{5... | collective-permute-start | bytes 245768 | tf_op jit(solution)/shard_map/ppermute | solution.py:252
  33.0 5.7 %collective-permute-start.16 = (f32[32,640]{1,0:T(8,128)S(1)}, f32[32,640]{1,0:T(8,128)S(1)}, u32[]{:S(2)}, u32[]{:S(2)}) collective-permute-start(f32[32,640]{1,0:T(8,128)S(1)} %add.110), channel_id=1, source_target_pairs={{0,24},{4,28},{8,16},{12,20},{16,8},{20,12},{24,0},{28,4},{1,25},{... | collective-permute-start | bytes 245768 | tf_op jit(solution)/shard_map/ppermute | solution.py:252
  35.6 4.6 %collective-permute-start.15 = (f32[32,640]{1,0:T(8,128)S(1)}, f32[32,640]{1,0:T(8,128)S(1)}, u32[]{:S(2)}, u32[]{:S(2)}) collective-permute-start(f32[32,640]{1,0:T(8,128)S(1)} %add.110), channel_id=1, source_target_pairs={{0,16},{4,20},{8,24},{12,28},{16,0},{20,4},{24,8},{28,12},{1,17},{... | collective-permute-start | bytes 245768 | tf_op jit(solution)/shard_map/ppermute | solution.py:252
  36.1 4.4 %collective-permute-start.14 = (f32[32,640]{1,0:T(8,128)S(1)}, f32[32,640]{1,0:T(8,128)S(1)}, u32[]{:S(2)}, u32[]{:S(2)}) collective-permute-start(f32[32,640]{1,0:T(8,128)S(1)} %add.110), channel_id=1, source_target_pairs={{0,8},{4,12},{8,0},{12,4},{16,24},{20,28},{24,16},{28,20},{1,9},{5... | collective-permute-start | bytes 245768 | tf_op jit(solution)/shard_map/ppermute | solution.py:252
  36.6 5.2 %collective-permute-start.19 = (f32[64,256]{1,0:T(8,128)S(1)}, f32[64,256]{1,0:T(8,128)S(1)}, u32[]{:S(2)}, u32[]{:S(2)}) collective-permute-start(f32[64,256]{1,0:T(8,128)S(1)} %fusion), channel_id=1, source_target_pairs={{0,2},{1,3},{2,0},{3,1},{4,6},{5,7},{6,4},{7,5},{8,10},{9,11},{10,... | collective-permute-start | bytes 196616 | tf_op jit(solution)/shard_map/ppermute | solution.py:252
  40.6 1.4 %collective-permute-start.17 = (f32[32,640]{1,0:T(8,128)S(1)}, f32[32,640]{1,0:T(8,128)S(1)}, u32[]{:S(2)}, u32[]{:S(2)}) collective-permute-start(f32[32,640]{1,0:T(8,128)S(1)} %multiply_add_fusion.own_ref), channel_id=1, source_target_pairs={{0,4},{4,0},{8,12},{12,8},{16,20},{20,16},{24,28},{28,24},{1,5},{5... | collective-permute-start | bytes 245768 | tf_op jit(solution)/shard_map/ppermute | solution.py:252
where the time goes:
time: 42.8 us; the launch traced here: 42.7 us
  starting transfers between devices  23.4 us (55%)
  waiting for transfers between devices  11.3 us (26%)
  Pallas kernels  6.33 us (15%)
  between operations  0.88 us (2%)
  other arithmetic  0.57 us (1%)
    ppermute x20, starting transfers between devices, swap(): return lax.ppermute(x, axis, [(j, j ^ bits) for j in range(n)])  23.4 us
    ppermute x20, waiting for transfers between devices, swap(): return lax.ppermute(x, axis, [(j, j ^ bits) for j in range(n)])  11.3 us
    pallas_call x1, Pallas kernels, forward_first(): pl.pallas_call(functools.partial(first_kernel, scale), out_shape=shapes,...  1.75 us
    pallas_call x4, Pallas kernels, part(): pl.pallas_call(functools.partial(part_kernel, scale), out_shape=jax.Shape...  1.15 us
    pallas_call x1, Pallas kernels, rates_of(): pl.pallas_call(functools.partial(rates_kernel, scale), out_shape=jax.Shap...  1.1 us
  transfers between devices with their start and end apart: 20, of which 11 were waited for; matrix products, arithmetic and copies ran while one was open for 2% of the time, Pallas kernels for 8%

commit v1 on v0

--- a/solution.py
+++ b/solution.py
@@ -180,37 +180,43 @@
     )(u, v, size)
 
 
-def data_kernel(scale, counts_ref, u_ref, out_ref):
+def data_kernel(scale, counts_ref, u_ref, high_ref, low_ref, out_ref, high_out, low_out):
     k = u_ref.shape[0]
     u_high, u_low = split(u_ref[...] * scale)
     both = dot(jnp.concatenate([u_high, u_low], 0), counts_ref[...], NN)
     out_ref[...] = both[:k] + both[k:]
-
-
-def data_part(counts, u, scale):
+    high_out[...] = high_ref[...].T
+    low_out[...] = low_ref[...].T
+
+
+def data_part(counts, u, high, low, scale):
     return pl.pallas_call(
         functools.partial(data_kernel, scale),
-        out_shape=jax.ShapeDtypeStruct((u.shape[0], counts.shape[1]), jnp.float32),
-        in_specs=[VMEM] * 2,
-        out_specs=VMEM,
+        out_shape=(
+            jax.ShapeDtypeStruct((u.shape[0], counts.shape[1]), jnp.float32),
+            jax.ShapeDtypeStruct(counts.shape, high.dtype),
+            jax.ShapeDtypeStruct(counts.shape, low.dtype),
+        ),
+        in_specs=[VMEM] * 4,
+        out_specs=(VMEM,) * 3,
         name="data_part",
         compiler_params=PARAMS,
-    )(counts, u)
+    )(counts, u, high, low)
 
 
 def part_kernel(scale, at_ref, u_ref, size_ref, data_ref, high_ref, low_ref, out_ref):
     hk = out_ref.shape[0]
     rows = pl.ds(pl.multiple_of(at_ref[0], hk), hk)
     u_high, u_low = split(u_ref[rows, :] * size_ref[...] * scale)
-    both = dot(jnp.concatenate([u_high, u_low], 0), high_ref[...], NT)
-    rest = dot(u_high, low_ref[...], NT)
+    both = dot(jnp.concatenate([u_high, u_low], 0), high_ref[...], NN)
+    rest = dot(u_high, low_ref[...], NN)
     out_ref[...] = data_ref[rows, :] - (both[:hk] + both[hk:] + rest)
 
 
 def part(at, u, size, data, high, low, scale):
     return pl.pallas_call(
         functools.partial(part_kernel, scale),
-        out_shape=jax.ShapeDtypeStruct((u.shape[0] // 2, high.shape[0]), jnp.float32),
+        out_shape=jax.ShapeDtypeStruct((u.shape[0] // 2, high.shape[1]), jnp.float32),
         in_specs=[SMEM] + [VMEM] * 5,
         out_specs=VMEM,
         compiler_params=PARAMS,
@@ -319,7 +325,7 @@
             pack, high, low = forward_again(factors, loads, scale)
         wide = products(counts_in, loads, high, low, scale)
         got, near, whole = gather(wide, pack)
-        data = data_part(counts_in, factors, scale)
+        data, high, low = data_part(counts_in, factors, high, low, scale)
         library = whole[1:2] if first else library
         size = library / whole[0:1]
         cross, own_size = cross_of(wide, got, pack, near, size)

time: 42.8 us -> 42.6 us (level)
  transfers between devices with their start and end apart: 20 -> 20, of which waited for: 11 -> 11; matrix products, arithmetic and copies ran while one was open for 2% -> 2% of each run, Pallas kernels for 8% -> 7%
where the time goes in v1:
time: 42.6 us; the launch traced here: 42.4 us
  starting transfers between devices  23.4 us (55%)
  waiting for transfers between devices  11.3 us (27%)
  Pallas kernels  6.13 us (14%)
  between operations  0.86 us (2%)
  other arithmetic  0.56 us (1%)
    ppermute x20, starting transfers between devices, swap(): return lax.ppermute(x, axis, [(j, j ^ bits) for j in range(n)])  23.4 us
    ppermute x20, waiting for transfers between devices, swap(): return lax.ppermute(x, axis, [(j, j ^ bits) for j in range(n)])  11.3 us
    pallas_call x1, Pallas kernels, forward_first(): pl.pallas_call(functools.partial(first_kernel, scale), out_shape=shapes,...  1.75 us
    pallas_call x1, Pallas kernels, rates_of(): pl.pallas_call(functools.partial(rates_kernel, scale), out_shape=jax.Shap...  1.1 us
    pallas_call x4, Pallas kernels, part(): pl.pallas_call(functools.partial(part_kernel, scale), out_shape=jax.Shape...  0.88 us
  transfers between devices with their start and end apart: 20, of which 11 were waited for; matrix products, arithmetic and copies ran while one was open for 2% of the time, Pallas kernels for 7%

profile of v1, /device:TPU:0, one launch (start us, length us, event | category | flops | bytes accessed | tf_op | source)
XLA Modules:
  0.0 42.4 jit_solution(10906685416927510967)
XLA Ops:
  0.6 1.7 %forward_first.1 = (f32[8,256]{1,0:T(8,128)S(1)}, bf16[640,256]{1,0:T(8,128)(2,1)S(1)}, bf16[640,256]{1,0:T(8,128)(2,1)S(1)}, bf16[256,640]{1,0:T(8,128)(2,1)S(1...) custom-call(s32[256,640]{1,0:T(8,128)} %counts_hbm.1, f32[64,256]{1,0:T(8,128)} %u_hbm.1, ...), custom_call_target="tpu_custom_call" | custom-call | tf_op jit(solution)/shard_map/forward_first/pallas_call | solution.py:98
  2.4 5.1 %collective-permute-start.3 = (f32[8,256]{1,0:T(8,128)S(1)}, f32[8,256]{1,0:T(8,128)S(1)}, u32[]{:S(2)}, u32[]{:S(2)}) collective-permute-start(f32[8,256]{1,0:T(8,128)S(1)} %get-tuple-element.29), channel_id=1, source_target_pairs={{0,3},{1,2},{2,1},{3,0},{4,7},{5,6},{6,5},{7,4},{8,11},{9,10},{10,... | collective-permute-start | bytes 24584 | tf_op jit(solution)/shard_map/ppermute | solution.py:258
  7.5 0.0 collective-permute-start.2
  7.5 0.6 %collective-permute-start.1 = (f32[8,256]{1,0:T(8,128)S(1)}, f32[8,256]{1,0:T(8,128)S(1)}, u32[]{:S(2)}, u32[]{:S(2)}) collective-permute-start(f32[8,256]{1,0:T(8,128)S(1)} %get-tuple-element.29), channel_id=1, source_target_pairs={{0,1},{1,0},{2,3},{3,2},{4,5},{5,4},{6,7},{7,6},{8,9},{9,8},{10,11... | collective-permute-start | bytes 24584 | tf_op jit(solution)/shard_map/ppermute | solution.py:258
  8.2 0.3 products.2
  8.5 1.4 %collective-permute-start = (f32[128,256]{1,0:T(8,128)S(1)}, f32[128,256]{1,0:T(8,128)S(1)}, u32[]{:S(2)}, u32[]{:S(2)}) collective-permute-start(f32[128,256]{1,0:T(8,128)S(1)} %products.2), channel_id=1, source_target_pairs={{0,1},{1,0},{2,3},{3,2},{4,5},{5,4},{6,7},{7,6},{8,9},{9,8},{10,11... | collective-permute-start | bytes 393224 | tf_op jit(solution)/shard_map/ppermute | solution.py:258
  10.0 0.1 broadcast_multiply_fusion
  10.0 0.2 data_part.2
  10.3 0.0 collective-permute-done.3
  10.3 1.8 %collective-permute-done.2 = f32[8,256]{1,0:T(8,128)S(1)} collective-permute-done((f32[8,256]{1,0:T(8,128)S(1)}, f32[8,256]{1,0:T(8,128)S(1)}, u32[]{:S(2)}, u32[]{:S(2)}) %collective-permute-start.2) | collective-permute-done | bytes 8224 | tf_op jit(solution)/shard_map/ppermute | solution.py:258
  12.1 0.0 collective-permute-done.1
  12.1 0.2 shard_map.101
  12.4 0.1 collective-permute-start.5
  12.5 0.2 shard_map.102
  12.7 0.1 fusion.9
  12.8 0.9 %collective-permute-done.5 = f32[32,640]{1,0:T(8,128)S(1)} collective-permute-done((f32[32,640]{1,0:T(8,128)S(1)}, f32[32,640]{1,0:T(8,128)S(1)}, u32[]{:S(2)}, u32[]{:S(2)}) %collective-permute-start.5) | collective-permute-done | bytes 81952 | tf_op jit(solution)/shard_map/ppermute | solution.py:258
  13.7 2.5 %collective-permute-start.8 = (f32[32,640]{1,0:T(8,128)S(1)}, f32[32,640]{1,0:T(8,128)S(1)}, u32[]{:S(2)}, u32[]{:S(2)}) collective-permute-start(f32[32,640]{1,0:T(8,128)S(1)} %add.100), channel_id=1, source_target_pairs={{0,24},{4,28},{8,16},{12,20},{16,8},{20,12},{24,0},{28,4},{1,25},{... | collective-permute-start | bytes 245768 | tf_op jit(solution)/shard_map/ppermute | solution.py:258
  16.2 0.5 %collective-permute-start.7 = (f32[32,640]{1,0:T(8,128)S(1)}, f32[32,640]{1,0:T(8,128)S(1)}, u32[]{:S(2)}, u32[]{:S(2)}) collective-permute-start(f32[32,640]{1,0:T(8,128)S(1)} %add.100), channel_id=1, source_target_pairs={{0,16},{4,20},{8,24},{12,28},{16,0},{20,4},{24,8},{28,12},{1,17},{... | collective-permute-start | bytes 245768 | tf_op jit(solution)/shard_map/ppermute | solution.py:258
  16.7 0.5 %collective-permute-start.6 = (f32[32,640]{1,0:T(8,128)S(1)}, f32[32,640]{1,0:T(8,128)S(1)}, u32[]{:S(2)}, u32[]{:S(2)}) collective-permute-start(f32[32,640]{1,0:T(8,128)S(1)} %add.100), channel_id=1, source_target_pairs={{0,8},{4,12},{8,0},{12,4},{16,24},{20,28},{24,16},{28,20},{1,9},{5... | collective-permute-start | bytes 245768 | tf_op jit(solution)/shard_map/ppermute | solution.py:258
  17.3 0.0 collective-permute-done
  17.3 2.1 %collective-permute-start.4 = (f32[64,256]{1,0:T(8,128)S(1)}, f32[64,256]{1,0:T(8,128)S(1)}, u32[]{:S(2)}, u32[]{:S(2)}) collective-permute-start(f32[64,256]{1,0:T(8,128)S(1)} %fusion.2), channel_id=1, source_target_pairs={{0,2},{1,3},{2,0},{3,1},{4,6},{5,7},{6,4},{7,5},{8,10},{9,11},{10,... | collective-permute-start | bytes 196616 | tf_op jit(solution)/shard_map/ppermute | solution.py:258
  19.4 0.0 collective-permute-done.8
  19.4 1.5 %collective-permute-done.7 = f32[32,640]{1,0:T(8,128)S(1)} collective-permute-done((f32[32,640]{1,0:T(8,128)S(1)}, f32[32,640]{1,0:T(8,128)S(1)}, u32[]{:S(2)}, u32[]{:S(2)}) %collective-permute-start.7) | collective-permute-done | bytes 81952 | tf_op jit(solution)/shard_map/ppermute | solution.py:258
  20.9 0.2 collective-permute-done.6
  21.2 0.0 copy-done.3
  21.2 0.1 multiply_add_fusion.1
  21.3 0.1 collective-permute-start.9
  21.4 1.2 %collective-permute-done.4 = f32[64,256]{1,0:T(8,128)S(1)} collective-permute-done((f32[64,256]{1,0:T(8,128)S(1)}, f32[64,256]{1,0:T(8,128)S(1)}, u32[]{:S(2)}, u32[]{:S(2)}) %collective-permute-start.4) | collective-permute-done | bytes 65568 | tf_op jit(solution)/shard_map/ppermute | solution.py:258
  22.5 0.0 copy-done.2
  22.5 0.1 multiply_add_fusion.4.u_ref
  22.6 0.0 copy-start
  22.6 0.0 collective-permute-done.9
  22.7 0.0 copy-start.1
  22.7 0.5 %forward_again.1 = (f32[8,256]{1,0:T(8,128)S(1)}, bf16[640,256]{1,0:T(8,128)(2,1)S(1)}, bf16[640,256]{1,0:T(8,128)(2,1)S(1)}) custom-call(f32[64,256]{1,0:T(8,128)S(1)} %multiply_add_fusion.4.u_ref, f32[64,640]{1,0:T(8,128)S(1)} %pad_maximum_fusion.v_ref), custom_call_target="tpu_custom_call" | custom-call | tf_op jit(solution)/shard_map/forward_again/pallas_call | solution.py:119
  23.2 2.1 %collective-permute-start.12 = (f32[8,256]{1,0:T(8,128)S(1)}, f32[8,256]{1,0:T(8,128)S(1)}, u32[]{:S(2)}, u32[]{:S(2)}) collective-permute-start(f32[8,256]{1,0:T(8,128)S(1)} %get-tuple-element.33), channel_id=1, source_target_pairs={{0,3},{1,2},{2,1},{3,0},{4,7},{5,6},{6,5},{7,4},{8,11},{9,10},{10,... | collective-permute-start | bytes 24584 | tf_op jit(solution)/shard_map/ppermute | solution.py:258
  25.3 0.1 collective-permute-start.11
  25.5 2.2 %collective-permute-start.10 = (f32[8,256]{1,0:T(8,128)S(1)}, f32[8,256]{1,0:T(8,128)S(1)}, u32[]{:S(2)}, u32[]{:S(2)}) collective-permute-start(f32[8,256]{1,0:T(8,128)S(1)} %get-tuple-element.33), channel_id=1, source_target_pairs={{0,1},{1,0},{2,3},{3,2},{4,5},{5,4},{6,7},{7,6},{8,9},{9,8},{10,11... | collective-permute-start | bytes 24584 | tf_op jit(solution)/shard_map/ppermute | solution.py:258
  27.7 0.3 products.3
  28.0 0.2 data_part.3
  28.3 0.1 collective-permute-start.18
  28.4 0.4 %collective-permute-done.12 = f32[8,256]{1,0:T(8,128)S(1)} collective-permute-done((f32[8,256]{1,0:T(8,128)S(1)}, f32[8,256]{1,0:T(8,128)S(1)}, u32[]{:S(2)}, u32[]{:S(2)}) %collective-permute-start.12) | collective-permute-done | bytes 8224 | tf_op jit(solution)/shard_map/ppermute | solution.py:258
  28.8 1.1 %collective-permute-done.11 = f32[8,256]{1,0:T(8,128)S(1)} collective-permute-done((f32[8,256]{1,0:T(8,128)S(1)}, f32[8,256]{1,0:T(8,128)S(1)}, u32[]{:S(2)}, u32[]{:S(2)}) %collective-permute-start.11) | collective-permute-done | bytes 8224 | tf_op jit(solution)/shard_map/ppermute | solution.py:258
  29.9 0.0 collective-permute-done.10
  29.9 0.2 shard_map.103
  30.2 0.2 shard_map.104
  30.4 0.0 copy-done.1
  30.4 1.1 %rates.1 = bf16[256,640]{1,0:T(8,128)(2,1)} custom-call(f32[64,256]{1,0:T(8,128)S(1)} %multiply_add_fusion.4.u_ref, f32[64,640]{1,0:T(8,128)S(1)} %pad_maximum_fusion.v_ref, f32[1,256]{1,0:T(1,128)S(1)} %get-tuple-element.42.size_ref), custom_call_target="tpu_custom_call" | custom-call | tf_op jit(solution)/shard_map/rates/pallas_call | solution.py:173
  31.5 0.0 collective-permute-start.13
  31.5 0.1 fusion.10
  31.6 1.2 %collective-permute-done.13 = f32[32,640]{1,0:T(8,128)S(1)} collective-permute-done((f32[32,640]{1,0:T(8,128)S(1)}, f32[32,640]{1,0:T(8,128)S(1)}, u32[]{:S(2)}, u32[]{:S(2)}) %collective-permute-start.13) | collective-permute-done | bytes 81952 | tf_op jit(solution)/shard_map/ppermute | solution.py:258
  32.8 2.6 %collective-permute-start.16 = (f32[32,640]{1,0:T(8,128)S(1)}, f32[32,640]{1,0:T(8,128)S(1)}, u32[]{:S(2)}, u32[]{:S(2)}) collective-permute-start(f32[32,640]{1,0:T(8,128)S(1)} %add.110), channel_id=1, source_target_pairs={{0,24},{4,28},{8,16},{12,20},{16,8},{20,12},{24,0},{28,4},{1,25},{... | collective-permute-start | bytes 245768 | tf_op jit(solution)/shard_map/ppermute | solution.py:258
  35.4 0.4 collective-permute-start.15
  35.8 0.5 %collective-permute-start.14 = (f32[32,640]{1,0:T(8,128)S(1)}, f32[32,640]{1,0:T(8,128)S(1)}, u32[]{:S(2)}, u32[]{:S(2)}) collective-permute-start(f32[32,640]{1,0:T(8,128)S(1)} %add.110), channel_id=1, source_target_pairs={{0,8},{4,12},{8,0},{12,4},{16,24},{20,28},{24,16},{28,20},{1,9},{5... | collective-permute-start | bytes 245768 | tf_op jit(solution)/shard_map/ppermute | solution.py:258
  36.3 0.0 collective-permute-done.18
  36.4 2.2 %collective-permute-start.19 = (f32[64,256]{1,0:T(8,128)S(1)}, f32[64,256]{1,0:T(8,128)S(1)}, u32[]{:S(2)}, u32[]{:S(2)}) collective-permute-start(f32[64,256]{1,0:T(8,128)S(1)} %fusion), channel_id=1, source_target_pairs={{0,2},{1,3},{2,0},{3,1},{4,6},{5,7},{6,4},{7,5},{8,10},{9,11},{10,... | collective-permute-start | bytes 196616 | tf_op jit(solution)/shard_map/ppermute | solution.py:258
  38.5 0.0 collective-permute-done.16
  38.5 1.5 %collective-permute-done.15 = f32[32,640]{1,0:T(8,128)S(1)} collective-permute-done((f32[32,640]{1,0:T(8,128)S(1)}, f32[32,640]{1,0:T(8,128)S(1)}, u32[]{:S(2)}, u32[]{:S(2)}) %collective-permute-start.15) | collective-permute-done | bytes 81952 | tf_op jit(solution)/shard_map/ppermute | solution.py:258
  40.0 0.2 collective-permute-done.14
  40.3 0.1 multiply_add_fusion.own_ref
  40.3 0.1 collective-permute-start.17
  40.4 1.2 %collective-permute-done.19 = f32[64,256]{1,0:T(8,128)S(1)} collective-permute-done((f32[64,256]{1,0:T(8,128)S(1)}, f32[64,256]{1,0:T(8,128)S(1)}, u32[]{:S(2)}, u32[]{:S(2)}) %collective-permute-start.19) | collective-permute-done | bytes 65568 | tf_op jit(solution)/shard_map/ppermute | solution.py:258
  41.6 0.1 multiply_add_fusion.3.u_ref
  41.7 0.0 collective-permute-done.17.other_ref
  41.7 0.7 %finish.1 = (f32[64,256]{1,0:T(8,128)}, f32[64,640]{1,0:T(8,128)}) custom-call(s32[1]{0:T(128)} %bitcast.5.at_ref, f32[32,640]{1,0:T(8,128)S(1)} %multiply_add_fusion.own_ref, f32[32,640]{1,0:T(8,128)S(1)} %collective-permute-done.17.other_ref, f32[64,256]{1,0:T(8,128)S(1)} %multiply_add_fusion.3.u_ref), custom_call_target="tpu_custom_call" | custom-call | tf_op jit(solution)/shard_map/finish/pallas_call | solution.py:242
  (18 shorter events, 0.2 us)
Async XLA Ops:
  2.4 7.9 %collective-permute-start.3 = (f32[8,256]{1,0:T(8,128)S(1)}, f32[8,256]{1,0:T(8,128)S(1)}, u32[]{:S(2)}, u32[]{:S(2)}) collective-permute-start(f32[8,256]{1,0:T(8,128)S(1)} %get-tuple-element.29), channel_id=1, source_target_pairs={{0,3},{1,2},{2,1},{3,0},{4,7},{5,6},{6,5},{7,4},{8,11},{9,10},{10,... | collective-permute-start | bytes 24584 | tf_op jit(solution)/shard_map/ppermute | solution.py:258
  7.5 4.6 %collective-permute-start.2 = (f32[8,256]{1,0:T(8,128)S(1)}, f32[8,256]{1,0:T(8,128)S(1)}, u32[]{:S(2)}, u32[]{:S(2)}) collective-permute-start(f32[8,256]{1,0:T(8,128)S(1)} %get-tuple-element.29), channel_id=1, source_target_pairs={{0,2},{1,3},{2,0},{3,1},{4,6},{5,7},{6,4},{7,5},{8,10},{9,11},{10,... | collective-permute-start | bytes 24584 | tf_op jit(solution)/shard_map/ppermute | solution.py:258
  7.5 4.6 %collective-permute-start.1 = (f32[8,256]{1,0:T(8,128)S(1)}, f32[8,256]{1,0:T(8,128)S(1)}, u32[]{:S(2)}, u32[]{:S(2)}) collective-permute-start(f32[8,256]{1,0:T(8,128)S(1)} %get-tuple-element.29), channel_id=1, source_target_pairs={{0,1},{1,0},{2,3},{3,2},{4,5},{5,4},{6,7},{7,6},{8,9},{9,8},{10,11... | collective-permute-start | bytes 24584 | tf_op jit(solution)/shard_map/ppermute | solution.py:258
  8.5 8.8 %collective-permute-start = (f32[128,256]{1,0:T(8,128)S(1)}, f32[128,256]{1,0:T(8,128)S(1)}, u32[]{:S(2)}, u32[]{:S(2)}) collective-permute-start(f32[128,256]{1,0:T(8,128)S(1)} %products.2), channel_id=1, source_target_pairs={{0,1},{1,0},{2,3},{3,2},{4,5},{5,4},{6,7},{7,6},{8,9},{9,8},{10,11... | collective-permute-start | bytes 393224 | tf_op jit(solution)/shard_map/ppermute | solution.py:258
  12.4 1.3 %collective-permute-start.5 = (f32[32,640]{1,0:T(8,128)S(1)}, f32[32,640]{1,0:T(8,128)S(1)}, u32[]{:S(2)}, u32[]{:S(2)}) collective-permute-start(f32[32,640]{1,0:T(8,128)S(1)} %shard_map.101), channel_id=1, source_target_pairs={{0,4},{4,0},{8,12},{12,8},{16,20},{20,16},{24,28},{28,24},{1,5},{5... | collective-permute-start | bytes 245768 | tf_op jit(solution)/shard_map/ppermute | solution.py:258
  13.7 5.7 %collective-permute-start.8 = (f32[32,640]{1,0:T(8,128)S(1)}, f32[32,640]{1,0:T(8,128)S(1)}, u32[]{:S(2)}, u32[]{:S(2)}) collective-permute-start(f32[32,640]{1,0:T(8,128)S(1)} %add.100), channel_id=1, source_target_pairs={{0,24},{4,28},{8,16},{12,20},{16,8},{20,12},{24,0},{28,4},{1,25},{... | collective-permute-start | bytes 245768 | tf_op jit(solution)/shard_map/ppermute | solution.py:258
  16.2 4.7 %collective-permute-start.7 = (f32[32,640]{1,0:T(8,128)S(1)}, f32[32,640]{1,0:T(8,128)S(1)}, u32[]{:S(2)}, u32[]{:S(2)}) collective-permute-start(f32[32,640]{1,0:T(8,128)S(1)} %add.100), channel_id=1, source_target_pairs={{0,16},{4,20},{8,24},{12,28},{16,0},{20,4},{24,8},{28,12},{1,17},{... | collective-permute-start | bytes 245768 | tf_op jit(solution)/shard_map/ppermute | solution.py:258
  16.7 4.4 %collective-permute-start.6 = (f32[32,640]{1,0:T(8,128)S(1)}, f32[32,640]{1,0:T(8,128)S(1)}, u32[]{:S(2)}, u32[]{:S(2)}) collective-permute-start(f32[32,640]{1,0:T(8,128)S(1)} %add.100), channel_id=1, source_target_pairs={{0,8},{4,12},{8,0},{12,4},{16,24},{20,28},{24,16},{28,20},{1,9},{5... | collective-permute-start | bytes 245768 | tf_op jit(solution)/shard_map/ppermute | solution.py:258
  17.3 3.9 %copy-start.3 = (f32[64,640]{1,0:T(8,128)S(1)}, f32[64,640]{1,0:T(8,128)}, u32[]{:S(2)}) copy-start(f32[64,640]{1,0:T(8,128)} %param.10) | copy-start | bytes 491524
  17.3 5.2 %collective-permute-start.4 = (f32[64,256]{1,0:T(8,128)S(1)}, f32[64,256]{1,0:T(8,128)S(1)}, u32[]{:S(2)}, u32[]{:S(2)}) collective-permute-start(f32[64,256]{1,0:T(8,128)S(1)} %fusion.2), channel_id=1, source_target_pairs={{0,2},{1,3},{2,0},{3,1},{4,6},{5,7},{6,4},{7,5},{8,10},{9,11},{10,... | collective-permute-start | bytes 196616 | tf_op jit(solution)/shard_map/ppermute | solution.py:258
  21.2 1.3 %copy-start.2 = (f32[64,256]{1,0:T(8,128)S(1)}, f32[64,256]{1,0:T(8,128)}, u32[]{:S(2)}) copy-start(f32[64,256]{1,0:T(8,128)} %param.9) | copy-start | bytes 196612
  21.3 1.4 %collective-permute-start.9 = (f32[32,640]{1,0:T(8,128)S(1)}, f32[32,640]{1,0:T(8,128)S(1)}, u32[]{:S(2)}, u32[]{:S(2)}) collective-permute-start(f32[32,640]{1,0:T(8,128)S(1)} %get-tuple-element.43), channel_id=1, source_target_pairs={{0,4},{4,0},{8,12},{12,8},{16,20},{20,16},{24,28},{28,24},{1,5},{5... | collective-permute-start | bytes 245768 | tf_op jit(solution)/shard_map/ppermute | solution.py:258
  22.6 19.0 %copy-start = (f32[64,256]{1,0:T(8,128)}, f32[64,256]{1,0:T(8,128)S(1)}, u32[]{:S(2)}) copy-start(f32[64,256]{1,0:T(8,128)S(1)} %multiply_add_fusion.4.u_ref) | copy-start | bytes 196612
  22.7 7.7 %copy-start.1 = (f32[64,640]{1,0:T(8,128)}, f32[64,640]{1,0:T(8,128)S(1)}, u32[]{:S(2)}) copy-start(f32[64,640]{1,0:T(8,128)S(1)} %pad_maximum_fusion.v_ref) | copy-start | bytes 491524
  23.2 5.6 %collective-permute-start.12 = (f32[8,256]{1,0:T(8,128)S(1)}, f32[8,256]{1,0:T(8,128)S(1)}, u32[]{:S(2)}, u32[]{:S(2)}) collective-permute-start(f32[8,256]{1,0:T(8,128)S(1)} %get-tuple-element.33), channel_id=1, source_target_pairs={{0,3},{1,2},{2,1},{3,0},{4,7},{5,6},{6,5},{7,4},{8,11},{9,10},{10,... | collective-permute-start | bytes 24584 | tf_op jit(solution)/shard_map/ppermute | solution.py:258
  25.3 4.6 %collective-permute-start.11 = (f32[8,256]{1,0:T(8,128)S(1)}, f32[8,256]{1,0:T(8,128)S(1)}, u32[]{:S(2)}, u32[]{:S(2)}) collective-permute-start(f32[8,256]{1,0:T(8,128)S(1)} %get-tuple-element.33), channel_id=1, source_target_pairs={{0,2},{1,3},{2,0},{3,1},{4,6},{5,7},{6,4},{7,5},{8,10},{9,11},{10,... | collective-permute-start | bytes 24584 | tf_op jit(solution)/shard_map/ppermute | solution.py:258
  25.5 4.4 %collective-permute-start.10 = (f32[8,256]{1,0:T(8,128)S(1)}, f32[8,256]{1,0:T(8,128)S(1)}, u32[]{:S(2)}, u32[]{:S(2)}) collective-permute-start(f32[8,256]{1,0:T(8,128)S(1)} %get-tuple-element.33), channel_id=1, source_target_pairs={{0,1},{1,0},{2,3},{3,2},{4,5},{5,4},{6,7},{7,6},{8,9},{9,8},{10,11... | collective-permute-start | bytes 24584 | tf_op jit(solution)/shard_map/ppermute | solution.py:258
  28.3 8.1 %collective-permute-start.18 = (f32[128,256]{1,0:T(8,128)S(1)}, f32[128,256]{1,0:T(8,128)S(1)}, u32[]{:S(2)}, u32[]{:S(2)}) collective-permute-start(f32[128,256]{1,0:T(8,128)S(1)} %products.3), channel_id=1, source_target_pairs={{0,1},{1,0},{2,3},{3,2},{4,5},{5,4},{6,7},{7,6},{8,9},{9,8},{10,11... | collective-permute-start | bytes 393224 | tf_op jit(solution)/shard_map/ppermute | solution.py:258
  31.5 1.3 %collective-permute-start.13 = (f32[32,640]{1,0:T(8,128)S(1)}, f32[32,640]{1,0:T(8,128)S(1)}, u32[]{:S(2)}, u32[]{:S(2)}) collective-permute-start(f32[32,640]{1,0:T(8,128)S(1)} %shard_map.103), channel_id=1, source_target_pairs={{0,4},{4,0},{8,12},{12,8},{16,20},{20,16},{24,28},{28,24},{1,5},{5... | collective-permute-start | bytes 245768 | tf_op jit(solution)/shard_map/ppermute | solution.py:258
  32.8 5.7 %collective-permute-start.16 = (f32[32,640]{1,0:T(8,128)S(1)}, f32[32,640]{1,0:T(8,128)S(1)}, u32[]{:S(2)}, u32[]{:S(2)}) collective-permute-start(f32[32,640]{1,0:T(8,128)S(1)} %add.110), channel_id=1, source_target_pairs={{0,24},{4,28},{8,16},{12,20},{16,8},{20,12},{24,0},{28,4},{1,25},{... | collective-permute-start | bytes 245768 | tf_op jit(solution)/shard_map/ppermute | solution.py:258
  35.4 4.6 %collective-permute-start.15 = (f32[32,640]{1,0:T(8,128)S(1)}, f32[32,640]{1,0:T(8,128)S(1)}, u32[]{:S(2)}, u32[]{:S(2)}) collective-permute-start(f32[32,640]{1,0:T(8,128)S(1)} %add.110), channel_id=1, source_target_pairs={{0,16},{4,20},{8,24},{12,28},{16,0},{20,4},{24,8},{28,12},{1,17},{... | collective-permute-start | bytes 245768 | tf_op jit(solution)/shard_map/ppermute | solution.py:258
  35.8 4.4 %collective-permute-start.14 = (f32[32,640]{1,0:T(8,128)S(1)}, f32[32,640]{1,0:T(8,128)S(1)}, u32[]{:S(2)}, u32[]{:S(2)}) collective-permute-start(f32[32,640]{1,0:T(8,128)S(1)} %add.110), channel_id=1, source_target_pairs={{0,8},{4,12},{8,0},{12,4},{16,24},{20,28},{24,16},{28,20},{1,9},{5... | collective-permute-start | bytes 245768 | tf_op jit(solution)/shard_map/ppermute | solution.py:258
  36.4 5.2 %collective-permute-start.19 = (f32[64,256]{1,0:T(8,128)S(1)}, f32[64,256]{1,0:T(8,128)S(1)}, u32[]{:S(2)}, u32[]{:S(2)}) collective-permute-start(f32[64,256]{1,0:T(8,128)S(1)} %fusion), channel_id=1, source_target_pairs={{0,2},{1,3},{2,0},{3,1},{4,6},{5,7},{6,4},{7,5},{8,10},{9,11},{10,... | collective-permute-start | bytes 196616 | tf_op jit(solution)/shard_map/ppermute | solution.py:258
  40.3 1.4 %collective-permute-start.17 = (f32[32,640]{1,0:T(8,128)S(1)}, f32[32,640]{1,0:T(8,128)S(1)}, u32[]{:S(2)}, u32[]{:S(2)}) collective-permute-start(f32[32,640]{1,0:T(8,128)S(1)} %multiply_add_fusion.own_ref), channel_id=1, source_target_pairs={{0,4},{4,0},{8,12},{12,8},{16,20},{20,16},{24,28},{28,24},{1,5},{5... | collective-permute-start | bytes 245768 | tf_op jit(solution)/shard_map/ppermute | solution.py:258

commit v2 on v1

--- a/solution.py
+++ b/solution.py
@@ -180,13 +180,14 @@
     )(u, v, size)
 
 
-def data_kernel(scale, counts_ref, u_ref, high_ref, low_ref, out_ref, high_out, low_out):
+def data_kernel(scale, counts_ref, u_ref, high_ref, low_ref, out_ref, both_out):
     k = u_ref.shape[0]
     u_high, u_low = split(u_ref[...] * scale)
     both = dot(jnp.concatenate([u_high, u_low], 0), counts_ref[...], NN)
     out_ref[...] = both[:k] + both[k:]
-    high_out[...] = high_ref[...].T
-    low_out[...] = low_ref[...].T
+    cells = counts_ref.shape[0]
+    both_out[0:cells, :] = high_ref[...].T
+    both_out[cells:, :] = low_ref[...].T
 
 
 def data_part(counts, u, high, low, scale):
@@ -194,33 +195,32 @@
         functools.partial(data_kernel, scale),
         out_shape=(
             jax.ShapeDtypeStruct((u.shape[0], counts.shape[1]), jnp.float32),
-            jax.ShapeDtypeStruct(counts.shape, high.dtype),
-            jax.ShapeDtypeStruct(counts.shape, low.dtype),
+            jax.ShapeDtypeStruct((2 * counts.shape[0], counts.shape[1]), high.dtype),
         ),
         in_specs=[VMEM] * 4,
-        out_specs=(VMEM,) * 3,
+        out_specs=(VMEM,) * 2,
         name="data_part",
         compiler_params=PARAMS,
     )(counts, u, high, low)
 
 
-def part_kernel(scale, at_ref, u_ref, size_ref, data_ref, high_ref, low_ref, out_ref):
+def part_kernel(scale, at_ref, u_ref, size_ref, data_ref, probs_ref, out_ref):
     hk = out_ref.shape[0]
     rows = pl.ds(pl.multiple_of(at_ref[0], hk), hk)
     u_high, u_low = split(u_ref[rows, :] * size_ref[...] * scale)
-    both = dot(jnp.concatenate([u_high, u_low], 0), high_ref[...], NN)
-    rest = dot(u_high, low_ref[...], NN)
-    out_ref[...] = data_ref[rows, :] - (both[:hk] + both[hk:] + rest)
-
-
-def part(at, u, size, data, high, low, scale):
+    u_both = jnp.concatenate([u_high, u_low], 0)
+    both = dot(jnp.concatenate([u_both, u_both], 1), probs_ref[...], NN)
+    out_ref[...] = data_ref[rows, :] - (both[:hk] + both[hk:])
+
+
+def part(at, u, size, data, probs, scale):
     return pl.pallas_call(
         functools.partial(part_kernel, scale),
-        out_shape=jax.ShapeDtypeStruct((u.shape[0] // 2, high.shape[1]), jnp.float32),
-        in_specs=[SMEM] + [VMEM] * 5,
+        out_shape=jax.ShapeDtypeStruct((u.shape[0] // 2, probs.shape[1]), jnp.float32),
+        in_specs=[SMEM] + [VMEM] * 4,
         out_specs=VMEM,
         compiler_params=PARAMS,
-    )(at, u, size, data, high, low)
+    )(at, u, size, data, probs)
 
 
 def finish_kernel(at_ref, own_ref, other_ref, u_ref, u_hbm, v_hbm, sems):
@@ -325,13 +325,13 @@
             pack, high, low = forward_again(factors, loads, scale)
         wide = products(counts_in, loads, high, low, scale)
         got, near, whole = gather(wide, pack)
-        data, high, low = data_part(counts_in, factors, high, low, scale)
+        data, probs = data_part(counts_in, factors, high, low, scale)
         library = whole[1:2] if first else library
         size = library / whole[0:1]
         cross, own_size = cross_of(wide, got, pack, near, size)
-        send = part(at_send, factors, own_size, data, high, low, scale)
+        send = part(at_send, factors, own_size, data, probs, scale)
         back = swap(send, "cell", 1)
-        kept = part(at_own, factors, own_size, data, high, low, scale)
+        kept = part(at_own, factors, own_size, data, probs, scale)
         total = exchange_sum(back + kept, "cell", 2)
         ard = (genes_total + 2.0) / (whole[2, :k] + 2.0)
         own = mine(loads) if first else own

time: 42.6 us -> 42.7 us (level)
  transfers between devices with their start and end apart: 20 -> 20, of which waited for: 11 -> 11; matrix products, arithmetic and copies ran while one was open for 2% -> 2% of each run, Pallas kernels for 7% -> 8%
where the time goes in v2:
time: 42.7 us; the launch traced here: 42.5 us
  starting transfers between devices  23.4 us (55%)
  waiting for transfers between devices  11.3 us (26%)
  Pallas kernels  6.2 us (15%)
  between operations  0.89 us (2%)
  other arithmetic  0.56 us (1%)
    ppermute x20, starting transfers between devices, swap(): return lax.ppermute(x, axis, [(j, j ^ bits) for j in range(n)])  23.4 us
    ppermute x20, waiting for transfers between devices, swap(): return lax.ppermute(x, axis, [(j, j ^ bits) for j in range(n)])  11.3 us
    pallas_call x1, Pallas kernels, forward_first(): pl.pallas_call(functools.partial(first_kernel, scale), out_shape=shapes,...  1.75 us
    pallas_call x1, Pallas kernels, rates_of(): pl.pallas_call(functools.partial(rates_kernel, scale), out_shape=jax.Shap...  1.1 us
    pallas_call x4, Pallas kernels, part(): pl.pallas_call(functools.partial(part_kernel, scale), out_shape=jax.Shape...  0.95 us
  transfers between devices with their start and end apart: 20, of which 11 were waited for; matrix products, arithmetic and copies ran while one was open for 2% of the time, Pallas kernels for 8%

profile of v2, /device:TPU:0, one launch (start us, length us, event | category | flops | bytes accessed | tf_op | source)
XLA Modules:
  0.0 42.5 jit_solution(16491771935942471857)
XLA Ops:
  0.6 1.7 %forward_first.1 = (f32[8,256]{1,0:T(8,128)S(1)}, bf16[640,256]{1,0:T(8,128)(2,1)S(1)}, bf16[640,256]{1,0:T(8,128)(2,1)S(1)}, bf16[256,640]{1,0:T(8,128)(2,1)S(1...) custom-call(s32[256,640]{1,0:T(8,128)} %counts_hbm.1, f32[64,256]{1,0:T(8,128)} %u_hbm.1, ...), custom_call_target="tpu_custom_call" | custom-call | tf_op jit(solution)/shard_map/forward_first/pallas_call | solution.py:98
  2.4 5.1 %collective-permute-start.3 = (f32[8,256]{1,0:T(8,128)S(1)}, f32[8,256]{1,0:T(8,128)S(1)}, u32[]{:S(2)}, u32[]{:S(2)}) collective-permute-start(f32[8,256]{1,0:T(8,128)S(1)} %get-tuple-element.27), channel_id=1, source_target_pairs={{0,3},{1,2},{2,1},{3,0},{4,7},{5,6},{6,5},{7,4},{8,11},{9,10},{10,... | collective-permute-start | bytes 24584 | tf_op jit(solution)/shard_map/ppermute | solution.py:258
  7.5 0.0 collective-permute-start.2
  7.5 0.6 %collective-permute-start.1 = (f32[8,256]{1,0:T(8,128)S(1)}, f32[8,256]{1,0:T(8,128)S(1)}, u32[]{:S(2)}, u32[]{:S(2)}) collective-permute-start(f32[8,256]{1,0:T(8,128)S(1)} %get-tuple-element.27), channel_id=1, source_target_pairs={{0,1},{1,0},{2,3},{3,2},{4,5},{5,4},{6,7},{7,6},{8,9},{9,8},{10,11... | collective-permute-start | bytes 24584 | tf_op jit(solution)/shard_map/ppermute | solution.py:258
  8.2 0.3 products.2
  8.5 1.4 %collective-permute-start = (f32[128,256]{1,0:T(8,128)S(1)}, f32[128,256]{1,0:T(8,128)S(1)}, u32[]{:S(2)}, u32[]{:S(2)}) collective-permute-start(f32[128,256]{1,0:T(8,128)S(1)} %products.2), channel_id=1, source_target_pairs={{0,1},{1,0},{2,3},{3,2},{4,5},{5,4},{6,7},{7,6},{8,9},{9,8},{10,11... | collective-permute-start | bytes 393224 | tf_op jit(solution)/shard_map/ppermute | solution.py:258
  10.0 0.1 broadcast_multiply_fusion
  10.0 0.2 data_part.2
  10.3 0.0 collective-permute-done.3
  10.3 1.8 %collective-permute-done.2 = f32[8,256]{1,0:T(8,128)S(1)} collective-permute-done((f32[8,256]{1,0:T(8,128)S(1)}, f32[8,256]{1,0:T(8,128)S(1)}, u32[]{:S(2)}, u32[]{:S(2)}) %collective-permute-start.2) | collective-permute-done | bytes 8224 | tf_op jit(solution)/shard_map/ppermute | solution.py:258
  12.1 0.0 collective-permute-done.1
  12.1 0.2 shard_map.101
  12.4 0.1 collective-permute-start.5
  12.5 0.2 shard_map.102
  12.7 0.1 fusion.9
  12.8 0.9 %collective-permute-done.5 = f32[32,640]{1,0:T(8,128)S(1)} collective-permute-done((f32[32,640]{1,0:T(8,128)S(1)}, f32[32,640]{1,0:T(8,128)S(1)}, u32[]{:S(2)}, u32[]{:S(2)}) %collective-permute-start.5) | collective-permute-done | bytes 81952 | tf_op jit(solution)/shard_map/ppermute | solution.py:258
  13.7 2.5 %collective-permute-start.8 = (f32[32,640]{1,0:T(8,128)S(1)}, f32[32,640]{1,0:T(8,128)S(1)}, u32[]{:S(2)}, u32[]{:S(2)}) collective-permute-start(f32[32,640]{1,0:T(8,128)S(1)} %add.100), channel_id=1, source_target_pairs={{0,24},{4,28},{8,16},{12,20},{16,8},{20,12},{24,0},{28,4},{1,25},{... | collective-permute-start | bytes 245768 | tf_op jit(solution)/shard_map/ppermute | solution.py:258
  16.2 0.5 %collective-permute-start.7 = (f32[32,640]{1,0:T(8,128)S(1)}, f32[32,640]{1,0:T(8,128)S(1)}, u32[]{:S(2)}, u32[]{:S(2)}) collective-permute-start(f32[32,640]{1,0:T(8,128)S(1)} %add.100), channel_id=1, source_target_pairs={{0,16},{4,20},{8,24},{12,28},{16,0},{20,4},{24,8},{28,12},{1,17},{... | collective-permute-start | bytes 245768 | tf_op jit(solution)/shard_map/ppermute | solution.py:258
  16.8 0.5 %collective-permute-start.6 = (f32[32,640]{1,0:T(8,128)S(1)}, f32[32,640]{1,0:T(8,128)S(1)}, u32[]{:S(2)}, u32[]{:S(2)}) collective-permute-start(f32[32,640]{1,0:T(8,128)S(1)} %add.100), channel_id=1, source_target_pairs={{0,8},{4,12},{8,0},{12,4},{16,24},{20,28},{24,16},{28,20},{1,9},{5... | collective-permute-start | bytes 245768 | tf_op jit(solution)/shard_map/ppermute | solution.py:258
  17.3 0.0 collective-permute-done
  17.3 2.1 %collective-permute-start.4 = (f32[64,256]{1,0:T(8,128)S(1)}, f32[64,256]{1,0:T(8,128)S(1)}, u32[]{:S(2)}, u32[]{:S(2)}) collective-permute-start(f32[64,256]{1,0:T(8,128)S(1)} %fusion.2), channel_id=1, source_target_pairs={{0,2},{1,3},{2,0},{3,1},{4,6},{5,7},{6,4},{7,5},{8,10},{9,11},{10,... | collective-permute-start | bytes 196616 | tf_op jit(solution)/shard_map/ppermute | solution.py:258
  19.5 0.0 collective-permute-done.8
  19.5 1.5 %collective-permute-done.7 = f32[32,640]{1,0:T(8,128)S(1)} collective-permute-done((f32[32,640]{1,0:T(8,128)S(1)}, f32[32,640]{1,0:T(8,128)S(1)}, u32[]{:S(2)}, u32[]{:S(2)}) %collective-permute-start.7) | collective-permute-done | bytes 81952 | tf_op jit(solution)/shard_map/ppermute | solution.py:258
  21.0 0.2 collective-permute-done.6
  21.2 0.0 copy-done.3
  21.2 0.1 multiply_add_fusion.1
  21.3 0.1 collective-permute-start.9
  21.4 1.2 %collective-permute-done.4 = f32[64,256]{1,0:T(8,128)S(1)} collective-permute-done((f32[64,256]{1,0:T(8,128)S(1)}, f32[64,256]{1,0:T(8,128)S(1)}, u32[]{:S(2)}, u32[]{:S(2)}) %collective-permute-start.4) | collective-permute-done | bytes 65568 | tf_op jit(solution)/shard_map/ppermute | solution.py:258
  22.6 0.0 copy-done.2
  22.6 0.1 multiply_add_fusion.4.u_ref
  22.6 0.0 copy-start
  22.7 0.0 collective-permute-done.9
  22.7 0.0 copy-start.1
  22.7 0.5 %forward_again.1 = (f32[8,256]{1,0:T(8,128)S(1)}, bf16[640,256]{1,0:T(8,128)(2,1)S(1)}, bf16[640,256]{1,0:T(8,128)(2,1)S(1)}) custom-call(f32[64,256]{1,0:T(8,128)S(1)} %multiply_add_fusion.4.u_ref, f32[64,640]{1,0:T(8,128)S(1)} %pad_maximum_fusion.v_ref), custom_call_target="tpu_custom_call" | custom-call | tf_op jit(solution)/shard_map/forward_again/pallas_call | solution.py:119
  23.3 2.1 %collective-permute-start.12 = (f32[8,256]{1,0:T(8,128)S(1)}, f32[8,256]{1,0:T(8,128)S(1)}, u32[]{:S(2)}, u32[]{:S(2)}) collective-permute-start(f32[8,256]{1,0:T(8,128)S(1)} %get-tuple-element.30), channel_id=1, source_target_pairs={{0,3},{1,2},{2,1},{3,0},{4,7},{5,6},{6,5},{7,4},{8,11},{9,10},{10,... | collective-permute-start | bytes 24584 | tf_op jit(solution)/shard_map/ppermute | solution.py:258
  25.4 0.1 collective-permute-start.11
  25.5 2.2 %collective-permute-start.10 = (f32[8,256]{1,0:T(8,128)S(1)}, f32[8,256]{1,0:T(8,128)S(1)}, u32[]{:S(2)}, u32[]{:S(2)}) collective-permute-start(f32[8,256]{1,0:T(8,128)S(1)} %get-tuple-element.30), channel_id=1, source_target_pairs={{0,1},{1,0},{2,3},{3,2},{4,5},{5,4},{6,7},{7,6},{8,9},{9,8},{10,11... | collective-permute-start | bytes 24584 | tf_op jit(solution)/shard_map/ppermute | solution.py:258
  27.7 0.3 products.3
  28.1 0.2 data_part.3
  28.3 0.1 collective-permute-start.18
  28.4 0.4 %collective-permute-done.12 = f32[8,256]{1,0:T(8,128)S(1)} collective-permute-done((f32[8,256]{1,0:T(8,128)S(1)}, f32[8,256]{1,0:T(8,128)S(1)}, u32[]{:S(2)}, u32[]{:S(2)}) %collective-permute-start.12) | collective-permute-done | bytes 8224 | tf_op jit(solution)/shard_map/ppermute | solution.py:258
  28.8 1.1 %collective-permute-done.11 = f32[8,256]{1,0:T(8,128)S(1)} collective-permute-done((f32[8,256]{1,0:T(8,128)S(1)}, f32[8,256]{1,0:T(8,128)S(1)}, u32[]{:S(2)}, u32[]{:S(2)}) %collective-permute-start.11) | collective-permute-done | bytes 8224 | tf_op jit(solution)/shard_map/ppermute | solution.py:258
  29.9 0.0 collective-permute-done.10
  30.0 0.2 shard_map.103
  30.2 0.2 shard_map.104
  30.5 0.0 copy-done.1
  30.5 1.1 %rates.1 = bf16[256,640]{1,0:T(8,128)(2,1)} custom-call(f32[64,256]{1,0:T(8,128)S(1)} %multiply_add_fusion.4.u_ref, f32[64,640]{1,0:T(8,128)S(1)} %pad_maximum_fusion.v_ref, f32[1,256]{1,0:T(1,128)S(1)} %get-tuple-element.38.size_ref), custom_call_target="tpu_custom_call" | custom-call | tf_op jit(solution)/shard_map/rates/pallas_call | solution.py:173
  31.6 0.0 collective-permute-start.13
  31.6 0.1 fusion.10
  31.6 1.2 %collective-permute-done.13 = f32[32,640]{1,0:T(8,128)S(1)} collective-permute-done((f32[32,640]{1,0:T(8,128)S(1)}, f32[32,640]{1,0:T(8,128)S(1)}, u32[]{:S(2)}, u32[]{:S(2)}) %collective-permute-start.13) | collective-permute-done | bytes 81952 | tf_op jit(solution)/shard_map/ppermute | solution.py:258
  32.9 2.6 %collective-permute-start.16 = (f32[32,640]{1,0:T(8,128)S(1)}, f32[32,640]{1,0:T(8,128)S(1)}, u32[]{:S(2)}, u32[]{:S(2)}) collective-permute-start(f32[32,640]{1,0:T(8,128)S(1)} %add.110), channel_id=1, source_target_pairs={{0,24},{4,28},{8,16},{12,20},{16,8},{20,12},{24,0},{28,4},{1,25},{... | collective-permute-start | bytes 245768 | tf_op jit(solution)/shard_map/ppermute | solution.py:258
  35.5 0.4 collective-permute-start.15
  35.9 0.5 %collective-permute-start.14 = (f32[32,640]{1,0:T(8,128)S(1)}, f32[32,640]{1,0:T(8,128)S(1)}, u32[]{:S(2)}, u32[]{:S(2)}) collective-permute-start(f32[32,640]{1,0:T(8,128)S(1)} %add.110), channel_id=1, source_target_pairs={{0,8},{4,12},{8,0},{12,4},{16,24},{20,28},{24,16},{28,20},{1,9},{5... | collective-permute-start | bytes 245768 | tf_op jit(solution)/shard_map/ppermute | solution.py:258
  36.4 0.0 collective-permute-done.18
  36.4 2.2 %collective-permute-start.19 = (f32[64,256]{1,0:T(8,128)S(1)}, f32[64,256]{1,0:T(8,128)S(1)}, u32[]{:S(2)}, u32[]{:S(2)}) collective-permute-start(f32[64,256]{1,0:T(8,128)S(1)} %fusion), channel_id=1, source_target_pairs={{0,2},{1,3},{2,0},{3,1},{4,6},{5,7},{6,4},{7,5},{8,10},{9,11},{10,... | collective-permute-start | bytes 196616 | tf_op jit(solution)/shard_map/ppermute | solution.py:258
  38.6 0.0 collective-permute-done.16
  38.6 1.5 %collective-permute-done.15 = f32[32,640]{1,0:T(8,128)S(1)} collective-permute-done((f32[32,640]{1,0:T(8,128)S(1)}, f32[32,640]{1,0:T(8,128)S(1)}, u32[]{:S(2)}, u32[]{:S(2)}) %collective-permute-start.15) | collective-permute-done | bytes 81952 | tf_op jit(solution)/shard_map/ppermute | solution.py:258
  40.1 0.2 collective-permute-done.14
  40.3 0.1 multiply_add_fusion.own_ref
  40.4 0.1 collective-permute-start.17
  40.5 1.2 %collective-permute-done.19 = f32[64,256]{1,0:T(8,128)S(1)} collective-permute-done((f32[64,256]{1,0:T(8,128)S(1)}, f32[64,256]{1,0:T(8,128)S(1)}, u32[]{:S(2)}, u32[]{:S(2)}) %collective-permute-start.19) | collective-permute-done | bytes 65568 | tf_op jit(solution)/shard_map/ppermute | solution.py:258
  41.7 0.1 multiply_add_fusion.3.u_ref
  41.8 0.0 collective-permute-done.17.other_ref
  41.8 0.7 %finish.1 = (f32[64,256]{1,0:T(8,128)}, f32[64,640]{1,0:T(8,128)}) custom-call(s32[1]{0:T(128)} %bitcast.5.at_ref, f32[32,640]{1,0:T(8,128)S(1)} %multiply_add_fusion.own_ref, f32[32,640]{1,0:T(8,128)S(1)} %collective-permute-done.17.other_ref, f32[64,256]{1,0:T(8,128)S(1)} %multiply_add_fusion.3.u_ref), custom_call_target="tpu_custom_call" | custom-call | tf_op jit(solution)/shard_map/finish/pallas_call | solution.py:242
  (18 shorter events, 0.2 us)
Async XLA Ops:
  2.4 7.9 %collective-permute-start.3 = (f32[8,256]{1,0:T(8,128)S(1)}, f32[8,256]{1,0:T(8,128)S(1)}, u32[]{:S(2)}, u32[]{:S(2)}) collective-permute-start(f32[8,256]{1,0:T(8,128)S(1)} %get-tuple-element.27), channel_id=1, source_target_pairs={{0,3},{1,2},{2,1},{3,0},{4,7},{5,6},{6,5},{7,4},{8,11},{9,10},{10,... | collective-permute-start | bytes 24584 | tf_op jit(solution)/shard_map/ppermute | solution.py:258
  7.5 4.6 %collective-permute-start.2 = (f32[8,256]{1,0:T(8,128)S(1)}, f32[8,256]{1,0:T(8,128)S(1)}, u32[]{:S(2)}, u32[]{:S(2)}) collective-permute-start(f32[8,256]{1,0:T(8,128)S(1)} %get-tuple-element.27), channel_id=1, source_target_pairs={{0,2},{1,3},{2,0},{3,1},{4,6},{5,7},{6,4},{7,5},{8,10},{9,11},{10,... | collective-permute-start | bytes 24584 | tf_op jit(solution)/shard_map/ppermute | solution.py:258
  7.5 4.6 %collective-permute-start.1 = (f32[8,256]{1,0:T(8,128)S(1)}, f32[8,256]{1,0:T(8,128)S(1)}, u32[]{:S(2)}, u32[]{:S(2)}) collective-permute-start(f32[8,256]{1,0:T(8,128)S(1)} %get-tuple-element.27), channel_id=1, source_target_pairs={{0,1},{1,0},{2,3},{3,2},{4,5},{5,4},{6,7},{7,6},{8,9},{9,8},{10,11... | collective-permute-start | bytes 24584 | tf_op jit(solution)/shard_map/ppermute | solution.py:258
  8.5 8.8 %collective-permute-start = (f32[128,256]{1,0:T(8,128)S(1)}, f32[128,256]{1,0:T(8,128)S(1)}, u32[]{:S(2)}, u32[]{:S(2)}) collective-permute-start(f32[128,256]{1,0:T(8,128)S(1)} %products.2), channel_id=1, source_target_pairs={{0,1},{1,0},{2,3},{3,2},{4,5},{5,4},{6,7},{7,6},{8,9},{9,8},{10,11... | collective-permute-start | bytes 393224 | tf_op jit(solution)/shard_map/ppermute | solution.py:258
  12.4 1.3 %collective-permute-start.5 = (f32[32,640]{1,0:T(8,128)S(1)}, f32[32,640]{1,0:T(8,128)S(1)}, u32[]{:S(2)}, u32[]{:S(2)}) collective-permute-start(f32[32,640]{1,0:T(8,128)S(1)} %shard_map.101), channel_id=1, source_target_pairs={{0,4},{4,0},{8,12},{12,8},{16,20},{20,16},{24,28},{28,24},{1,5},{5... | collective-permute-start | bytes 245768 | tf_op jit(solution)/shard_map/ppermute | solution.py:258
  13.7 5.7 %collective-permute-start.8 = (f32[32,640]{1,0:T(8,128)S(1)}, f32[32,640]{1,0:T(8,128)S(1)}, u32[]{:S(2)}, u32[]{:S(2)}) collective-permute-start(f32[32,640]{1,0:T(8,128)S(1)} %add.100), channel_id=1, source_target_pairs={{0,24},{4,28},{8,16},{12,20},{16,8},{20,12},{24,0},{28,4},{1,25},{... | collective-permute-start | bytes 245768 | tf_op jit(solution)/shard_map/ppermute | solution.py:258
  16.2 4.7 %collective-permute-start.7 = (f32[32,640]{1,0:T(8,128)S(1)}, f32[32,640]{1,0:T(8,128)S(1)}, u32[]{:S(2)}, u32[]{:S(2)}) collective-permute-start(f32[32,640]{1,0:T(8,128)S(1)} %add.100), channel_id=1, source_target_pairs={{0,16},{4,20},{8,24},{12,28},{16,0},{20,4},{24,8},{28,12},{1,17},{... | collective-permute-start | bytes 245768 | tf_op jit(solution)/shard_map/ppermute | solution.py:258
  16.8 4.4 %collective-permute-start.6 = (f32[32,640]{1,0:T(8,128)S(1)}, f32[32,640]{1,0:T(8,128)S(1)}, u32[]{:S(2)}, u32[]{:S(2)}) collective-permute-start(f32[32,640]{1,0:T(8,128)S(1)} %add.100), channel_id=1, source_target_pairs={{0,8},{4,12},{8,0},{12,4},{16,24},{20,28},{24,16},{28,20},{1,9},{5... | collective-permute-start | bytes 245768 | tf_op jit(solution)/shard_map/ppermute | solution.py:258
  17.3 3.9 %copy-start.3 = (f32[64,640]{1,0:T(8,128)S(1)}, f32[64,640]{1,0:T(8,128)}, u32[]{:S(2)}) copy-start(f32[64,640]{1,0:T(8,128)} %param.10) | copy-start | bytes 491524
  17.3 5.2 %collective-permute-start.4 = (f32[64,256]{1,0:T(8,128)S(1)}, f32[64,256]{1,0:T(8,128)S(1)}, u32[]{:S(2)}, u32[]{:S(2)}) collective-permute-start(f32[64,256]{1,0:T(8,128)S(1)} %fusion.2), channel_id=1, source_target_pairs={{0,2},{1,3},{2,0},{3,1},{4,6},{5,7},{6,4},{7,5},{8,10},{9,11},{10,... | collective-permute-start | bytes 196616 | tf_op jit(solution)/shard_map/ppermute | solution.py:258
  21.2 1.4 %copy-start.2 = (f32[64,256]{1,0:T(8,128)S(1)}, f32[64,256]{1,0:T(8,128)}, u32[]{:S(2)}) copy-start(f32[64,256]{1,0:T(8,128)} %param.9) | copy-start | bytes 196612
  21.3 1.4 %collective-permute-start.9 = (f32[32,640]{1,0:T(8,128)S(1)}, f32[32,640]{1,0:T(8,128)S(1)}, u32[]{:S(2)}, u32[]{:S(2)}) collective-permute-start(f32[32,640]{1,0:T(8,128)S(1)} %get-tuple-element.39), channel_id=1, source_target_pairs={{0,4},{4,0},{8,12},{12,8},{16,20},{20,16},{24,28},{28,24},{1,5},{5... | collective-permute-start | bytes 245768 | tf_op jit(solution)/shard_map/ppermute | solution.py:258
  22.6 19.1 %copy-start = (f32[64,256]{1,0:T(8,128)}, f32[64,256]{1,0:T(8,128)S(1)}, u32[]{:S(2)}) copy-start(f32[64,256]{1,0:T(8,128)S(1)} %multiply_add_fusion.4.u_ref) | copy-start | bytes 196612
  22.7 7.7 %copy-start.1 = (f32[64,640]{1,0:T(8,128)}, f32[64,640]{1,0:T(8,128)S(1)}, u32[]{:S(2)}) copy-start(f32[64,640]{1,0:T(8,128)S(1)} %pad_maximum_fusion.v_ref) | copy-start | bytes 491524
  23.3 5.6 %collective-permute-start.12 = (f32[8,256]{1,0:T(8,128)S(1)}, f32[8,256]{1,0:T(8,128)S(1)}, u32[]{:S(2)}, u32[]{:S(2)}) collective-permute-start(f32[8,256]{1,0:T(8,128)S(1)} %get-tuple-element.30), channel_id=1, source_target_pairs={{0,3},{1,2},{2,1},{3,0},{4,7},{5,6},{6,5},{7,4},{8,11},{9,10},{10,... | collective-permute-start | bytes 24584 | tf_op jit(solution)/shard_map/ppermute | solution.py:258
  25.4 4.6 %collective-permute-start.11 = (f32[8,256]{1,0:T(8,128)S(1)}, f32[8,256]{1,0:T(8,128)S(1)}, u32[]{:S(2)}, u32[]{:S(2)}) collective-permute-start(f32[8,256]{1,0:T(8,128)S(1)} %get-tuple-element.30), channel_id=1, source_target_pairs={{0,2},{1,3},{2,0},{3,1},{4,6},{5,7},{6,4},{7,5},{8,10},{9,11},{10,... | collective-permute-start | bytes 24584 | tf_op jit(solution)/shard_map/ppermute | solution.py:258
  25.5 4.4 %collective-permute-start.10 = (f32[8,256]{1,0:T(8,128)S(1)}, f32[8,256]{1,0:T(8,128)S(1)}, u32[]{:S(2)}, u32[]{:S(2)}) collective-permute-start(f32[8,256]{1,0:T(8,128)S(1)} %get-tuple-element.30), channel_id=1, source_target_pairs={{0,1},{1,0},{2,3},{3,2},{4,5},{5,4},{6,7},{7,6},{8,9},{9,8},{10,11... | collective-permute-start | bytes 24584 | tf_op jit(solution)/shard_map/ppermute | solution.py:258
  28.3 8.1 %collective-permute-start.18 = (f32[128,256]{1,0:T(8,128)S(1)}, f32[128,256]{1,0:T(8,128)S(1)}, u32[]{:S(2)}, u32[]{:S(2)}) collective-permute-start(f32[128,256]{1,0:T(8,128)S(1)} %products.3), channel_id=1, source_target_pairs={{0,1},{1,0},{2,3},{3,2},{4,5},{5,4},{6,7},{7,6},{8,9},{9,8},{10,11... | collective-permute-start | bytes 393224 | tf_op jit(solution)/shard_map/ppermute | solution.py:258
  31.6 1.3 %collective-permute-start.13 = (f32[32,640]{1,0:T(8,128)S(1)}, f32[32,640]{1,0:T(8,128)S(1)}, u32[]{:S(2)}, u32[]{:S(2)}) collective-permute-start(f32[32,640]{1,0:T(8,128)S(1)} %shard_map.103), channel_id=1, source_target_pairs={{0,4},{4,0},{8,12},{12,8},{16,20},{20,16},{24,28},{28,24},{1,5},{5... | collective-permute-start | bytes 245768 | tf_op jit(solution)/shard_map/ppermute | solution.py:258
  32.9 5.7 %collective-permute-start.16 = (f32[32,640]{1,0:T(8,128)S(1)}, f32[32,640]{1,0:T(8,128)S(1)}, u32[]{:S(2)}, u32[]{:S(2)}) collective-permute-start(f32[32,640]{1,0:T(8,128)S(1)} %add.110), channel_id=1, source_target_pairs={{0,24},{4,28},{8,16},{12,20},{16,8},{20,12},{24,0},{28,4},{1,25},{... | collective-permute-start | bytes 245768 | tf_op jit(solution)/shard_map/ppermute | solution.py:258
  35.5 4.6 %collective-permute-start.15 = (f32[32,640]{1,0:T(8,128)S(1)}, f32[32,640]{1,0:T(8,128)S(1)}, u32[]{:S(2)}, u32[]{:S(2)}) collective-permute-start(f32[32,640]{1,0:T(8,128)S(1)} %add.110), channel_id=1, source_target_pairs={{0,16},{4,20},{8,24},{12,28},{16,0},{20,4},{24,8},{28,12},{1,17},{... | collective-permute-start | bytes 245768 | tf_op jit(solution)/shard_map/ppermute | solution.py:258
  35.9 4.4 %collective-permute-start.14 = (f32[32,640]{1,0:T(8,128)S(1)}, f32[32,640]{1,0:T(8,128)S(1)}, u32[]{:S(2)}, u32[]{:S(2)}) collective-permute-start(f32[32,640]{1,0:T(8,128)S(1)} %add.110), channel_id=1, source_target_pairs={{0,8},{4,12},{8,0},{12,4},{16,24},{20,28},{24,16},{28,20},{1,9},{5... | collective-permute-start | bytes 245768 | tf_op jit(solution)/shard_map/ppermute | solution.py:258
  36.4 5.3 %collective-permute-start.19 = (f32[64,256]{1,0:T(8,128)S(1)}, f32[64,256]{1,0:T(8,128)S(1)}, u32[]{:S(2)}, u32[]{:S(2)}) collective-permute-start(f32[64,256]{1,0:T(8,128)S(1)} %fusion), channel_id=1, source_target_pairs={{0,2},{1,3},{2,0},{3,1},{4,6},{5,7},{6,4},{7,5},{8,10},{9,11},{10,... | collective-permute-start | bytes 196616 | tf_op jit(solution)/shard_map/ppermute | solution.py:258
  40.4 1.4 %collective-permute-start.17 = (f32[32,640]{1,0:T(8,128)S(1)}, f32[32,640]{1,0:T(8,128)S(1)}, u32[]{:S(2)}, u32[]{:S(2)}) collective-permute-start(f32[32,640]{1,0:T(8,128)S(1)} %multiply_add_fusion.own_ref), channel_id=1, source_target_pairs={{0,4},{4,0},{8,12},{12,8},{16,20},{20,16},{24,28},{28,24},{1,5},{5... | collective-permute-start | bytes 245768 | tf_op jit(solution)/shard_map/ppermute | solution.py:258
